TPU v7x, 512 devices: a whole 4x8x8 slice. The times are simulated.
512 devices in a mesh: branch: 64 (over x, z_lo, y), head: 8 (over z_hi, core).
Axes of the slice: x: 4, y: 8, z: 8 (z_hi: 4, z_lo: 2; z = z_hi * 2 + z_lo), core: 2. Of those that a mesh axis runs over, the one named last changes fastest.
Arguments:
- queries: bfloat16 [16384, 8192], P('branch', 'head'), may hold values from -8 to 8
- branch_keys: bfloat16 [16384, 1024], P('branch', 'head'), may hold values from -6 to 6
- branch_values: bfloat16 [16384, 1024], P('branch', 'head'), may hold values from -6 to 6
- prompt_keys: bfloat16 [3072, 1024], P(('branch', 'head')), may hold values from -6 to 6
- prompt_values: bfloat16 [3072, 1024], P(('branch', 'head')), may hold values from -6 to 6
- parent: int32 [64], replicated, may hold values from -1 to 63, as said below
- fork_tokens: int32 [64], replicated, may hold values from 0 to 256, as said below
- lengths: int32 [64], replicated, may hold values from 64 to 256
Outputs:
- attended: bfloat16 [16384, 8192], P('branch', 'head')
Inputs may be any that keep to these rules, and one draw needn't show every extreme that they name: Exactly 8 branches have parent -1, and every other branch's parent is one of them. `fork_tokens`: 0 where parent is -1, else at most the parent's length.
All inputs are finite; a program needn't handle non-finite values.
Results may differ from a plain program's by a relative error of at most 0.0045.
Values may be sent and summed in bfloat16 or wider, within the bound.
No kernel may reach another device: no remote copies, remote signals or barrier semaphores. Data moves between devices by JAX's collectives and lax.ppermute only.
A program may use at most 64 MiB of HBM per device.

v0:
```python
import math

import jax
import jax.numpy as jnp
from jax import lax
from jax.sharding import PartitionSpec as P

HEADS = 64
KV_HEADS = 8
HEAD_DIM = 128


floor_score = -1e30


def sent_together(arrays, axis, dim, along):
    both = jnp.concatenate(arrays, axis=along)
    whole, at, gathered = (lax.all_gather(both, axis, axis=dim, tiled=True), 0, [])
    for a in arrays:
        gathered.append(lax.slice_in_dim(whole, at, at + a.shape[along], axis=along))
        at += a.shape[along]
    return tuple(gathered)


def body(
    queries, branch_keys, branch_values, prompt_keys, prompt_values, parent, fork_tokens, lengths
):
    tok_rows = queries.shape[0]
    groups = branch_keys.shape[1] // HEAD_DIM
    per_group = HEADS // KV_HEADS
    score_scale = 1.0 / math.sqrt(HEAD_DIM)
    query_block = queries.reshape(tok_rows, groups, per_group, HEAD_DIM)
    branch_index = lax.axis_index("branch")
    my_parent = parent[branch_index]
    parent_safe = jnp.maximum(my_parent, 0)
    my_fork = fork_tokens[branch_index]
    my_length = lengths[branch_index]
    query_pos = jnp.arange(tok_rows, dtype=jnp.int32)

    def tree_visible(offset, count_rows, with_self):
        key_index = offset + jnp.arange(count_rows, dtype=jnp.int32)
        source = key_index // tok_rows
        key_pos = key_index % tok_rows
        from_parent = ((source == my_parent) & (key_pos < my_fork))[None, :]
        if with_self:
            from_self = (source == branch_index)[None, :] & (key_pos[None, :] <= query_pos[:, None])
            return from_parent | from_self
        return jnp.broadcast_to(from_parent, (tok_rows, count_rows))

    def absorb(running, key_rows, value_rows, offset, masking):
        total_rows = key_rows.shape[0]
        block_rows = min(512, total_rows)
        padding = -total_rows % block_rows
        block_count = (total_rows + padding) // block_rows

        def advance(block_number, state):
            maxima, totals, accumulated = state
            begin = block_number * block_rows
            key_block = lax.dynamic_slice_in_dim(key_rows, begin, block_rows, 0).reshape(
                block_rows, groups, HEAD_DIM
            )
            value_block = lax.dynamic_slice_in_dim(value_rows, begin, block_rows, 0).reshape(
                block_rows, groups, HEAD_DIM
            )
            scores = (
                jnp.einsum(
                    "tgqd,ngd->tgqn", query_block, key_block, preferred_element_type=jnp.float32
                )
                * score_scale
            )
            masked = masking > 0 or padding > 0
            if masked:
                in_range = (begin + jnp.arange(block_rows, dtype=jnp.int32) < total_rows)[None, :]
                visible = tree_visible(offset + begin, block_rows, masking == 1) & in_range
                visible = visible[:, None, None, :]
                scores = jnp.where(visible, scores, floor_score)
            new_max = jnp.maximum(maxima, jnp.max(scores, axis=-1))
            rescale = jnp.exp(maxima - new_max)
            weights = jnp.exp(scores - new_max[..., None])
            if masked:
                weights = jnp.where(visible, weights, 0.0)
            totals = totals * rescale + jnp.sum(weights, axis=-1)
            accumulated = accumulated * rescale[..., None] + jnp.einsum(
                "tgqn,ngd->tgqd",
                weights.astype(jnp.bfloat16),
                value_block,
                preferred_element_type=jnp.float32,
            )
            return (new_max, totals, accumulated)

        return lax.fori_loop(0, block_count, advance, running)

    initial = (
        jnp.full((tok_rows, groups, per_group), floor_score, jnp.float32),
        jnp.zeros((tok_rows, groups, per_group), jnp.float32),
        jnp.zeros((tok_rows, groups, per_group, HEAD_DIM), jnp.float32),
    )
    slab_keys, slab_values = (
        lax.all_to_all(prompt_keys, "head", split_axis=1, concat_axis=0, tiled=True),
        lax.all_to_all(prompt_values, "head", split_axis=1, concat_axis=0, tiled=True),
    )
    whole_keys, whole_values = sent_together((slab_keys, slab_values), "branch", 0, 1)
    running = absorb(initial, whole_keys, whole_values, 0, 0)
    running = absorb(running, branch_keys, branch_values, branch_index * tok_rows, 1)
    root_count = lax.axis_size("branch") // 8
    root_rank = jnp.cumsum((parent < 0).astype(jnp.int32)) - 1
    my_slot = root_rank[branch_index]
    holder = (jnp.arange(root_count, dtype=jnp.int32) == my_slot) & (my_parent < 0)
    one_hot = holder.astype(jnp.float32)
    stacked = jnp.stack([branch_keys, branch_values]).astype(jnp.float32)
    slot_buffer = one_hot[:, None, None, None] * stacked[None]
    summed = lax.psum(slot_buffer, "branch")
    chosen = lax.dynamic_index_in_dim(summed, root_rank[parent_safe], 0, keepdims=False).astype(
        jnp.bfloat16
    )
    running = absorb(running, chosen[0], chosen[1], parent_safe * tok_rows, 2)
    maxima, totals, accumulated = running
    output = accumulated / totals[..., None]
    live = (query_pos < my_length)[:, None, None, None]
    return (
        jnp.where(live, output, 0.0)
        .reshape(tok_rows, groups * per_group * HEAD_DIM)
        .astype(jnp.bfloat16)
    )


def solution(mesh):
    placed = (
        P("branch", "head"),
        P("branch", "head"),
        P("branch", "head"),
        P(("branch", "head"), None),
        P(("branch", "head"), None),
        P(),
        P(),
        P(),
    )
    return jax.shard_map(
        body, mesh=mesh, in_specs=placed, out_specs=P("branch", "head"), check_vma=False
    )
```

profile of v0, /device:TPU:8, one launch (start us, length us, event | category | flops | bytes accessed | tf_op | source)
XLA Modules:
  0.0 402.3 jit_solution(11744310682368633162)
XLA Ops:
  6.5 0.0 copy-start.5
  6.5 0.0 copy-start.6
  6.5 0.0 copy-start.2
  6.5 10.4 %all-to-all-start = ((bf16[6,8,128]{2,0,1:T(8,128)(2,1)}), bf16[6,8,128]{2,0,1:T(8,128)(2,1)S(1)}, u32[]{:S(2)}, u32[]{:S(2)}) async-start(bf16[6,8,128]{2,0,1:T(8,128)(2,1)} %bitcast.246), calls=%async_computation | async-start | bytes 32768 | tf_op jit(solution)/shard_map/all_to_all | solution.py:99
  17.0 1.2 dynamic_slice.42
  19.5 0.7 fusion.69
  20.2 0.1 copy.30
  20.3 0.1 reduce-window.9
  20.4 0.5 constant_dynamic-slice_fusion
  20.9 0.6 and_convert_fusion
  21.6 0.9 maximum_convert_fusion
  22.5 1.6 broadcast_multiply_fusion
  24.1 0.0 copy-done.5
  24.1 0.6 dynamic_slice.43
  24.7 0.2 all-to-all-done
  24.8 7.0 %all-to-all-start.1 = ((bf16[6,8,128]{2,0,1:T(8,128)(2,1)}), bf16[6,8,128]{2,0,1:T(8,128)(2,1)S(1)}, u32[]{:S(2)}, u32[]{:S(2)}) async-start(bf16[6,8,128]{2,0,1:T(8,128)(2,1)} %bitcast.3), calls=%async_computation.1 | async-start | bytes 32768 | tf_op jit(solution)/shard_map/all_to_all | solution.py:100
  31.9 0.0 all-gather.2.cloned.1.call-start
  31.9 1.2 and_and_fusion
  33.2 0.0 copy-done.6
  33.2 0.6 dynamic_slice.41
  35.0 0.0 copy-done.2
  35.0 0.2 copy.24
  35.2 0.3 copy.25
  36.1 3.6 all-to-all-done.1
  39.7 0.6 pad_maximum_fusion
  40.3 0.0 all-gather.2.cloned.1.call-update
  40.4 0.6 iota_compare_fusion.2
  40.9 327.4 %all-reduce.1 = bf16[8,2,256,128]{3,2,1,0:T(8,128)(2,1)S(1)} all-reduce(f32[8,2,256,128]{3,2,1,0:T(8,128)} %broadcast_multiply_fusion), channel_id=1, replica_groups=mesh['branch'=64,'head'=8] {'branch'}, use_global_device_ids=true, to_apply=%region_6.7 | all-reduce | flops 524288 | bytes 3145728 | tf_op jit(solution)/shard_map/psum | solution.py:112
  368.3 0.0 copy-start.3
  368.4 0.2 fusion.60
  368.6 1.8 bitcast_reduce_fusion.1
  370.4 0.0 copy-done.3
  370.4 1.8 fusion.26
  372.1 1.5 fusion.77
  373.6 15.6 %while.5 = (s32[]{:T(128)}, f32[256,1,8]{0,2,1:T(8,128)S(1)}, f32[256,1,8]{0,2,1:T(8,128)S(1)}, f32[256,1,8,128]{0,3,2,1:T(8,128)S(1)}, bf16[3072,128]{1,0:T(8,1...) while((s32[]{:T(128)}, f32[256,1,8]{0,2,1:T(8,128)S(1)}, ...), condition=%wide.region_3.0_spmd.clone, body=%wide.region_0.0_spmd.clone.sunk | while | flops 546058240 | bytes 15597751 | solution.py:91
  373.6 0.7 bitcast_reduce_fusion.3
  374.4 0.7 fusion.88
  375.1 1.1 fusion.89
  376.2 0.7 bitcast_reduce_fusion.3
  377.0 0.7 fusion.88
  377.7 1.1 fusion.89
  378.8 0.7 bitcast_reduce_fusion.3
  379.6 0.7 fusion.88
  380.3 1.1 fusion.89
  381.4 0.7 bitcast_reduce_fusion.3
  382.2 0.7 fusion.88
  382.9 1.1 fusion.89
  384.0 0.7 bitcast_reduce_fusion.3
  384.8 0.7 fusion.88
  385.5 1.1 fusion.89
  386.6 0.7 bitcast_reduce_fusion.3
  387.3 0.7 fusion.88
  388.1 1.1 fusion.89
  389.2 0.0 copy-start.1
  389.2 2.3 fusion.29
  391.6 0.0 copy-done.1
  391.6 0.0 copy-start
  391.6 0.0 copy-start.4
  391.6 0.7 convolution_bitcast_fusion
  392.3 0.8 copy-done
  393.2 0.5 fusion.27
  393.7 0.0 copy-done.4
  393.7 0.8 fusion.36
  394.5 1.0 copy.34
  (30 shorter events, 0.3 us)
Async XLA Ops:
  6.5 17.6 %copy-start.5 = (s32[64]{0:T(128)S(1)}, s32[64]{0:T(128)}, u32[]{:S(2)}) copy-start(s32[64]{0:T(128)} %param.16) | copy-start | bytes 772
  6.5 26.6 %copy-start.6 = (s32[64]{0:T(128)S(1)}, s32[64]{0:T(128)}, u32[]{:S(2)}) copy-start(s32[64]{0:T(128)} %param.17) | copy-start | bytes 772
  6.5 28.4 %copy-start.2 = (bf16[256,1024]{1,0:T(8,128)(2,1)S(1)}, bf16[256,1024]{1,0:T(8,128)(2,1)}, u32[]{:S(2)}) copy-start(bf16[256,1024]{1,0:T(8,128)(2,1)} %param.10) | copy-start | bytes 1572868
  6.5 18.3 %all-to-all-start = ((bf16[6,8,128]{2,0,1:T(8,128)(2,1)}), bf16[6,8,128]{2,0,1:T(8,128)(2,1)S(1)}, u32[]{:S(2)}, u32[]{:S(2)}) async-start(bf16[6,8,128]{2,0,1:T(8,128)(2,1)} %bitcast.246), calls=%async_computation | async-start | bytes 32768 | tf_op jit(solution)/shard_map/all_to_all | solution.py:99
  24.8 14.9 %all-to-all-start.1 = ((bf16[6,8,128]{2,0,1:T(8,128)(2,1)}), bf16[6,8,128]{2,0,1:T(8,128)(2,1)S(1)}, u32[]{:S(2)}, u32[]{:S(2)}) async-start(bf16[6,8,128]{2,0,1:T(8,128)(2,1)} %bitcast.3), calls=%async_computation.1 | async-start | bytes 32768 | tf_op jit(solution)/shard_map/all_to_all | solution.py:100
  31.9 340.3 %all-gather.2.cloned.1.call-start = ((), (), s32[]{:S(2)}) async-start(), calls=%async_computation.2 | async-start | bytes 1597440 | tf_op jit(solution)/shard_map/all_gather | solution.py:18
  368.3 2.1 copy-start.3
  389.2 2.4 copy-start.1
  391.6 1.6 copy-start
  391.6 2.1 copy-start.4
Sparse Core Ops, SparseCore 0:
  40.5 299.1 all-gather.1
where the time goes:
time: 403 us; the launch traced here: 402 us
  blocking collectives  327 us (81%)
  starting transfers between devices  17.5 us (4%)
  between operations  16.8 us (4%)
  matrix products  15.9 us (4%)
  other arithmetic  13.7 us (3%)
  local copies, waits for them, and re-layouts  6.88 us (2%)
    psum x1, blocking collectives, body(): summed = lax.psum(slot_buffer, 'branch')  327 us
    all_to_all x1, starting transfers between devices, body(): lax.all_to_all(prompt_keys, 'head', split_axis=1, concat_axis=0, tiled=True)  10.4 us
  transfers between devices with their start and end apart: 3, of which 2 were waited for; matrix products, arithmetic and copies ran while one was open for 3% of the time, Pallas kernels for 0%

commit v1 on v0

v1 whole, which is shorter than its diff:
```python
import math

import jax
import jax.numpy as jnp
from jax import lax
from jax.experimental import pallas as pl
from jax.experimental.pallas import tpu as pltpu
from jax.sharding import Mesh, PartitionSpec as P

HEADS = 64
KV_HEADS = 8
HEAD_DIM = 128
PER_GROUP = HEADS // KV_HEADS
SCALE2 = math.log2(math.e) / math.sqrt(HEAD_DIM)
NEG = -1e30
BRANCH = ("x", "zl", "y")
PLANE = ("x", "zl")
HEAD = ("zh", "c")
CONTRACT_LAST = (((1,), (1,)), ((), ()))
CONTRACT_MID = (((1,), (0,)), ((), ()))


def scores_of(q, k):
    return lax.dot_general(q, k, CONTRACT_LAST, preferred_element_type=jnp.float32)


def attend_kernel(meta, q_ref, prompt_ref, own_k, own_v, parent_ref, o_ref):
    tok = q_ref.shape[0]
    q = q_ref[...]
    groups, rows = prompt_ref.shape[0], prompt_ref.shape[1] // 2
    col = lax.broadcasted_iota(jnp.int32, (tok, tok), 1)
    row = lax.broadcasted_iota(jnp.int32, (tok, tok), 0)
    parts = []
    for i in range(groups):
        parts.append((scores_of(q, prompt_ref[i, :rows]), prompt_ref[i, rows:]))
    own = jnp.where(col <= row, scores_of(q, own_k[...]), NEG)
    parts.append((own, own_v[...]))
    up = jnp.where(col < meta[0], scores_of(q, parent_ref[:tok]), NEG)
    parts.append((up, parent_ref[tok:]))
    top = None
    for s, _ in parts:
        peak = jnp.max(s, axis=1, keepdims=True)
        top = peak if top is None else jnp.maximum(top, peak)
    total = jnp.zeros((tok, 1), jnp.float32)
    acc = jnp.zeros((tok, HEAD_DIM), jnp.float32)
    for s, v in parts:
        w = jnp.exp2((s - top) * SCALE2)
        total += jnp.sum(w, axis=1, keepdims=True)
        acc += lax.dot_general(
            w.astype(jnp.bfloat16), v, CONTRACT_MID, preferred_element_type=jnp.float32
        )
    live = lax.broadcasted_iota(jnp.int32, (tok, HEAD_DIM), 0) < meta[1]
    o_ref[...] = jnp.where(live, acc / total, 0.0).astype(o_ref.dtype)


def attend(meta, queries, prompt, own_k, own_v, parent_kv):
    tok, width = queries.shape
    whole = lambda a: pl.BlockSpec(a.shape, lambda h, *_: (0,) * a.ndim)
    head = pl.BlockSpec((tok, HEAD_DIM), lambda h, *_: (0, h))
    keys = prompt.shape[0] * prompt.shape[1] // 2 + 2 * tok
    return pl.pallas_call(
        attend_kernel,
        out_shape=jax.ShapeDtypeStruct((tok, width), jnp.bfloat16),
        grid_spec=pltpu.PrefetchScalarGridSpec(
            num_scalar_prefetch=1,
            grid=(width // HEAD_DIM,),
            in_specs=[head, whole(prompt), whole(own_k), whole(own_v), whole(parent_kv)],
            out_specs=head,
        ),
        compiler_params=pltpu.CompilerParams(vmem_limit_bytes=48 << 20),
        cost_estimate=pl.CostEstimate(
            flops=4 * tok * width * keys,
            transcendentals=tok * (width // HEAD_DIM) * keys,
            bytes_accessed=4 * tok * width + 4 * keys * HEAD_DIM,
        ),
    )(meta, queries, prompt, own_k, own_v, parent_kv)


def body(queries, branch_keys, branch_values, prompt_keys, prompt_values, parent, fork, lengths):
    tok = queries.shape[0]
    rows = prompt_keys.shape[0]
    ny = lax.axis_size("y")
    nh = lax.axis_size(HEAD)
    nb = lax.axis_size(BRANCH)
    me = lax.axis_index(BRANCH)

    own = jnp.concatenate([branch_keys, branch_values], 0).reshape(nb, 2 * tok // nb, HEAD_DIM)
    pieces = lax.all_to_all(own, BRANCH, split_axis=0, concat_axis=0, tiled=True)
    chosen = pieces.at[jnp.maximum(parent, 0)].get(mode="promise_in_bounds")
    parent_kv = lax.all_to_all(chosen, BRANCH, split_axis=0, concat_axis=0, tiled=True)
    parent_kv = parent_kv.reshape(2 * tok, HEAD_DIM)

    split = lambda a: a.reshape(rows, nh, HEAD_DIM).transpose(1, 0, 2)
    mine = jnp.concatenate([split(prompt_keys), split(prompt_values)], 1)
    spread = jnp.broadcast_to(mine[None], (ny,) + mine.shape).reshape(ny * nh, 2 * rows, HEAD_DIM)
    line = lax.all_to_all(spread, ("y",) + HEAD, split_axis=0, concat_axis=0, tiled=True)
    part = lambda a: a.reshape(ny * nh * rows, HEAD_DIM)
    line = jnp.concatenate([part(line[:, :rows]), part(line[:, rows:])], 0)
    plane = lax.axis_size(PLANE)
    spread = jnp.broadcast_to(line[None], (plane,) + line.shape)
    prompt = lax.all_to_all(spread, PLANE, split_axis=0, concat_axis=0, tiled=True)

    meta = jnp.stack([fork[me], lengths[me]])
    return attend(meta, queries, prompt, branch_keys, branch_values, parent_kv)


def solution(mesh):
    fine = Mesh(mesh.devices.reshape(4, 2, 8, 4, 2), BRANCH + HEAD)
    placed = (
        P(BRANCH, HEAD),
        P(BRANCH, HEAD),
        P(BRANCH, HEAD),
        P(BRANCH + HEAD, None),
        P(BRANCH + HEAD, None),
        P(),
        P(),
        P(),
    )
    return jax.shard_map(
        body, mesh=fine, in_specs=placed, out_specs=P(BRANCH, HEAD), check_vma=False
    )
```

time: 403 us -> 107 us (0.27)
  blocking collectives: 327 us -> 0 us
  waiting for transfers between devices: 3.8 us -> 50.4 us
  between operations: 16.8 us -> 0.11 us
  starting transfers between devices: 17.5 us -> 33.7 us
  matrix products: 15.9 us -> 0 us
  Pallas kernels: 0 us -> 13.8 us
  other arithmetic: 13.7 us -> 3.51 us
    psum x1 -> x0, blocking collectives: 327 us -> none  [body(): summed = lax.psum(slot_buffer, 'branch')]
    all_to_all x2 -> x4, waiting for transfers between devices: 3.78 us -> 50.4 us  [the longest x1 17.9 us: body(): lax.all_to_all(spread, PLANE, split_axis=0, concat_axis=0, tiled=True)]
    all_to_all x2 -> x4, starting transfers between devices: 17.5 us -> 33.7 us  [the longest x1 12.4 us: body(): lax.all_to_all(own, BRANCH, split_axis=0, concat_axis=0, tiled=True)]
    dot_general x16 -> x0, matrix products: 15.9 us -> none  [the longest x8 8.03 us: advance(): jnp.einsum('tgqn,ngd->tgqd', weights.astype(jnp.bfloat16), value_block, p...]
    pallas_call x0 -> x1, Pallas kernels: none -> 13.8 us  [attend(): pl.pallas_call(attend_kernel, out_shape=jax.ShapeDtypeStruct((tok, width)...]
    reduce_sum x8 -> x0, other arithmetic: 7.01 us -> none  [advance(): totals = totals * rescale + jnp.sum(weights, axis=-1)]
  transfers between devices with their start and end apart: 3 -> 4, of which waited for: 2 -> 4; matrix products, arithmetic and copies ran while one was open for 3% -> 5% of each run, Pallas kernels for 0% -> 0%
where the time goes in v1:
time: 107 us
  waiting for transfers between devices  50.4 us (47%)
  starting transfers between devices  33.7 us (31%)
  Pallas kernels  13.8 us (13%)
  local copies, waits for them, and re-layouts  5.46 us (5%)
  other arithmetic  3.51 us (3%)
    all_to_all x1, waiting for transfers between devices, body(): lax.all_to_all(spread, PLANE, split_axis=0, concat_axis=0, tiled=True)  17.9 us
    pallas_call x1, Pallas kernels, attend(): pl.pallas_call(attend_kernel, out_shape=jax.ShapeDtypeStruct((tok, width)...  13.8 us
    all_to_all x1, waiting for transfers between devices, body(): lax.all_to_all(spread, ('y',) + HEAD, split_axis=0, concat_axis=0, tiled=...  12.7 us
    all_to_all x1, starting transfers between devices, body(): lax.all_to_all(own, BRANCH, split_axis=0, concat_axis=0, tiled=True)  12.4 us
    all_to_all x1, starting transfers between devices, body(): lax.all_to_all(spread, ('y',) + HEAD, split_axis=0, concat_axis=0, tiled=...  11.6 us
    all_to_all x1, waiting for transfers between devices, body(): lax.all_to_all(chosen, BRANCH, split_axis=0, concat_axis=0, tiled=True)  10.2 us
    all_to_all x1, waiting for transfers between devices, body(): lax.all_to_all(own, BRANCH, split_axis=0, concat_axis=0, tiled=True)  9.64 us
    all_to_all x1, starting transfers between devices, body(): lax.all_to_all(chosen, BRANCH, split_axis=0, concat_axis=0, tiled=True)  5.99 us
  transfers between devices with their start and end apart: 4, of which 4 were waited for; matrix products, arithmetic and copies ran while one was open for 5% of the time, Pallas kernels for 0%

profile of v1, /device:TPU:8, one launch (start us, length us, event | category | flops | bytes accessed | tf_op | source)
XLA Modules:
  0.0 106.9 jit_solution(3431669075052694424)
XLA Ops:
  0.0 1.5 %maximum_bitcast_fusion = bf16[64,8,128]{2,1,0:T(8,128)(2,1)} fusion(bf16[256,128]{1,0:T(8,128)(2,1)} %own_v.1, bf16[256,128]{1,0:T(8,128)(2,1)} %own_k.1), kind=kLoop, calls=%fused_computation.2 | loop fusion | flops 262144 | bytes 262144 | tf_op jit(solution)/shard_map/reshape | solution.py:87
  1.5 12.4 %all-to-all-start.2 = ((bf16[64,8,128]{2,1,0:T(8,128)(2,1)}), bf16[64,8,128]{2,1,0:T(8,128)(2,1)S(1)}, u32[]{:S(2)}, u32[]{:S(2)}) async-start(bf16[64,8,128]{2,1,0:T(8,128)(2,1)} %maximum_bitcast_fusion), calls=%async_computation.2 | async-start | bytes 262144 | tf_op jit(solution)/shard_map/all_to_all | solution.py:88
  13.9 0.7 bitcast_bitcast_fusion
  14.7 9.6 %all-to-all-done.2 = bf16[64,8,128]{2,1,0:T(8,128)(2,1)S(1)} async-done(((bf16[64,8,128]{2,1,0:T(8,128)(2,1)}), bf16[64,8,128]{2,1,0:T(8,128)(2,1)S(1)}, u32[]{:S(2)}, u32[]{:S(2)}) %all-to-all-start.2) | async-done | bytes 131104 | tf_op jit(solution)/shard_map/all_to_all | solution.py:88
  24.3 0.7 broadcast_in_dim.6
  25.1 11.6 %all-to-all-start = ((bf16[64,12,128]{2,1,0:T(8,128)(2,1)}), bf16[64,12,128]{2,1,0:T(8,128)(2,1)S(1)}, u32[]{:S(2)}, u32[]{:S(2)}) async-start(bf16[64,12,128]{2,1,0:T(8,128)(2,1)} %bitcast.2), calls=%async_computation | async-start | bytes 524288 | tf_op jit(solution)/shard_map/all_to_all | solution.py:96
  36.6 0.7 broadcast_maximum_fusion
  37.3 1.3 %gather_fusion = bf16[64,8,128]{2,1,0:T(8,128)(2,1)} fusion(bf16[64,8,128]{2,1,0:T(8,128)(2,1)S(1)} %all-to-all-done.2, s32[1024]{0:T(1024)S(1)} %pad_clamp_fusion), kind=kCustom, calls=%fused_computation | custom fusion | bytes 262400 | tf_op jit(solution)/shard_map/gather | solution.py:89
  38.6 12.7 %all-to-all-done = bf16[64,12,128]{2,1,0:T(8,128)(2,1)S(1)} async-done(((bf16[64,12,128]{2,1,0:T(8,128)(2,1)}), bf16[64,12,128]{2,1,0:T(8,128)(2,1)S(1)}, u32[]{:S(2)}, u32[]{:S(2)}) %all-to-all-start) | async-done | bytes 196640 | tf_op jit(solution)/shard_map/all_to_all | solution.py:96
  51.2 6.0 %all-to-all-start.3 = ((bf16[64,8,128]{2,1,0:T(8,128)(2,1)}), bf16[64,8,128]{2,1,0:T(8,128)(2,1)S(1)}, u32[]{:S(2)}, u32[]{:S(2)}) async-start(bf16[64,8,128]{2,1,0:T(8,128)(2,1)} %gather_fusion), calls=%async_computation.3 | async-start | bytes 262144 | tf_op jit(solution)/shard_map/all_to_all | solution.py:90
  57.2 0.1 fusion
  57.4 10.2 %all-to-all-done.3 = bf16[64,8,128]{2,1,0:T(8,128)(2,1)S(1)} async-done(((bf16[64,8,128]{2,1,0:T(8,128)(2,1)}), bf16[64,8,128]{2,1,0:T(8,128)(2,1)S(1)}, u32[]{:S(2)}, u32[]{:S(2)}) %all-to-all-start.3) | async-done | bytes 131104 | tf_op jit(solution)/shard_map/all_to_all | solution.py:90
  67.6 1.4 %broadcast_in_dim.7 = bf16[8,768,128]{2,1,0:T(8,128)(2,1)} broadcast(bf16[768,128]{1,0:T(8,128)(2,1)S(1)} %pad_maximum_fusion), dimensions={1,2} | broadcast | bytes 1769472 | tf_op jit(solution)/shard_map/broadcast_in_dim | solution.py:100
  69.0 0.0 copy-start.3
  69.0 0.0 copy-start.4
  69.0 0.0 copy-start
  69.0 0.0 copy-start.1
  69.0 0.0 copy-start.2
  69.0 3.7 %all-to-all-start.1 = ((bf16[8,768,128]{2,1,0:T(8,128)(2,1)}), bf16[8,768,128]{2,1,0:T(8,128)(2,1)S(1)}, u32[]{:S(2)}, u32[]{:S(2)}) async-start(bf16[8,768,128]{2,1,0:T(8,128)(2,1)} %broadcast_in_dim.7), calls=%async_computation.1 | async-start | bytes 3145728 | tf_op jit(solution)/shard_map/all_to_all | solution.py:101
  72.8 0.0 copy-done.3
  72.8 0.6 dynamic_slice.6
  73.4 0.0 copy-done.4
  73.4 0.6 dynamic_slice.7
  74.0 1.3 %pad_add_fusion.meta = s32[2]{0:T(128)S(1)} fusion(s32[1]{0:T(128)} %dynamic_slice.7, s32[1]{0:T(128)} %dynamic_slice.6), kind=kLoop, calls=%fused_computation.7 | loop fusion | flops 2 | bytes 16 | tf_op jit(solution)/shard_map/stack | solution.py:103
  75.2 17.9 %all-to-all-done.1.prompt_ref = bf16[8,768,128]{2,1,0:T(8,128)(2,1)S(1)} async-done(((bf16[8,768,128]{2,1,0:T(8,128)(2,1)}), bf16[8,768,128]{2,1,0:T(8,128)(2,1)S(1)}, u32[]{:S(2)}, u32[]{:S(2)}) %all-to-all-start.1) | async-done | bytes 1572896 | tf_op jit(solution)/shard_map/all_to_all | solution.py:101
  93.2 0.0 copy-done
  93.2 0.0 copy-done.1
  93.2 0.0 copy-done.2
  93.2 13.8 %shard_map.82 = bf16[256,1024]{1,0:T(8,128)(2,1)} custom-call(s32[2]{0:T(128)S(1)} %pad_add_fusion.meta, bf16[256,1024]{1,0:T(8,128)(2,1)S(1)} %copy-done.2, bf16[8,768,128]{2,1,0:T(8,128)(2,1)S(1)} %all-to-all-done.1.prompt_ref, bf16[256,128]{1,0:T(8,128)(2,1)S(1)} %copy-done, bf16[256,128]{1,0:T(8,128)(2,1)S(1)} %copy-done.1, bf16[512,128]{1,0:T(8,128)(2,1)S(1)} %bitcast.14), custom_call_target="tpu_custom_call" | custom-call | flops 3758096384 | bytes 2883584 | tf_op jit(solution)/shard_map/pallas_call | solution.py:61
  (6 shorter events, 0.1 us)
Async XLA Ops:
  1.5 22.8 %all-to-all-start.2 = ((bf16[64,8,128]{2,1,0:T(8,128)(2,1)}), bf16[64,8,128]{2,1,0:T(8,128)(2,1)S(1)}, u32[]{:S(2)}, u32[]{:S(2)}) async-start(bf16[64,8,128]{2,1,0:T(8,128)(2,1)} %maximum_bitcast_fusion), calls=%async_computation.2 | async-start | bytes 262144 | tf_op jit(solution)/shard_map/all_to_all | solution.py:88
  25.1 26.2 %all-to-all-start = ((bf16[64,12,128]{2,1,0:T(8,128)(2,1)}), bf16[64,12,128]{2,1,0:T(8,128)(2,1)S(1)}, u32[]{:S(2)}, u32[]{:S(2)}) async-start(bf16[64,12,128]{2,1,0:T(8,128)(2,1)} %bitcast.2), calls=%async_computation | async-start | bytes 524288 | tf_op jit(solution)/shard_map/all_to_all | solution.py:96
  51.2 16.4 %all-to-all-start.3 = ((bf16[64,8,128]{2,1,0:T(8,128)(2,1)}), bf16[64,8,128]{2,1,0:T(8,128)(2,1)S(1)}, u32[]{:S(2)}, u32[]{:S(2)}) async-start(bf16[64,8,128]{2,1,0:T(8,128)(2,1)} %gather_fusion), calls=%async_computation.3 | async-start | bytes 262144 | tf_op jit(solution)/shard_map/all_to_all | solution.py:90
  69.0 3.8 %copy-start.3 = (s32[64]{0:T(128)S(1)}, s32[64]{0:T(128)}, u32[]{:S(2)}) copy-start(s32[64]{0:T(128)} %param.14) | copy-start | bytes 772
  69.0 4.4 %copy-start.4 = (s32[64]{0:T(128)S(1)}, s32[64]{0:T(128)}, u32[]{:S(2)}) copy-start(s32[64]{0:T(128)} %param.15) | copy-start | bytes 772
  69.0 24.1 %copy-start = (bf16[256,128]{1,0:T(8,128)(2,1)S(1)}, bf16[256,128]{1,0:T(8,128)(2,1)}, u32[]{:S(2)}) copy-start(bf16[256,128]{1,0:T(8,128)(2,1)} %own_k.1) | copy-start | bytes 196612
  69.0 24.1 %copy-start.1 = (bf16[256,128]{1,0:T(8,128)(2,1)S(1)}, bf16[256,128]{1,0:T(8,128)(2,1)}, u32[]{:S(2)}) copy-start(bf16[256,128]{1,0:T(8,128)(2,1)} %own_v.1) | copy-start | bytes 196612
  69.0 24.1 %copy-start.2 = (bf16[256,1024]{1,0:T(8,128)(2,1)S(1)}, bf16[256,1024]{1,0:T(8,128)(2,1)}, u32[]{:S(2)}) copy-start(bf16[256,1024]{1,0:T(8,128)(2,1)} %q_ref.1) | copy-start | bytes 1572868
  69.0 24.1 %all-to-all-start.1 = ((bf16[8,768,128]{2,1,0:T(8,128)(2,1)}), bf16[8,768,128]{2,1,0:T(8,128)(2,1)S(1)}, u32[]{:S(2)}, u32[]{:S(2)}) async-start(bf16[8,768,128]{2,1,0:T(8,128)(2,1)} %broadcast_in_dim.7), calls=%async_computation.1 | async-start | bytes 3145728 | tf_op jit(solution)/shard_map/all_to_all | solution.py:101

commit v2 on v1

v2 whole, which is shorter than its diff:
```python
import functools
import math

import jax
import jax.numpy as jnp
from jax import lax
from jax.experimental import pallas as pl
from jax.experimental.pallas import tpu as pltpu
from jax.sharding import Mesh, PartitionSpec as P

HEAD_DIM = 128
SCALE2 = math.log2(math.e) / math.sqrt(HEAD_DIM)
NEG = -1e30
CHUNK = 512
BRANCH = ("x", "zl", "y")
PLANE = ("x", "zl")
HEAD = ("zh", "c")
CONTRACT_LAST = (((1,), (1,)), ((), ()))
CONTRACT_MID = (((1,), (0,)), ((), ()))


def absorb(q, parts, state):
    for k, v, mask in parts:
        s = lax.dot_general(q, k, CONTRACT_LAST, preferred_element_type=jnp.float32)
        if mask is not None:
            s = jnp.where(mask, s, NEG)
        top = jnp.max(s, axis=1, keepdims=True)
        if state is not None:
            top = jnp.maximum(state[0], top)
        w = jnp.exp2((s - top) * SCALE2).astype(jnp.bfloat16)
        both = lax.dot_general(
            w,
            jnp.concatenate([v, jnp.ones_like(v)], 1),
            CONTRACT_MID,
            preferred_element_type=jnp.float32,
        )
        acc, total = both[:, :HEAD_DIM], both[:, HEAD_DIM:]
        if state is not None:
            fade = jnp.exp2((state[0] - top) * SCALE2)
            total += state[1] * fade
            acc += state[2] * fade
        state = (top, total, acc)
    return state


def stacked(ref):
    return jnp.concatenate(
        [ref[:, i : i + HEAD_DIM] for i in range(0, ref.shape[1], HEAD_DIM)], 0
    )


def store_state(state, acc_ref, stat_ref, heads):
    top, total, acc = state
    tok = acc_ref.shape[0]
    here = acc_ref.shape[1] // HEAD_DIM
    step = pl.program_id(0)
    lane = lax.broadcasted_iota(jnp.int32, (tok, HEAD_DIM), 1)
    stat = stat_ref[...]
    for i in range(here):
        at = slice(i * tok, (i + 1) * tok)
        acc_ref[:, i * HEAD_DIM : (i + 1) * HEAD_DIM] = acc[at]
        stat = jnp.where(lane == step * here + i, top[at], stat)
        stat = jnp.where(lane == heads + step * here + i, total[at], stat)
    stat_ref[...] = stat


def load_state(acc_ref, stat_ref, heads):
    here = acc_ref.shape[1] // HEAD_DIM
    step = pl.program_id(0)
    stat = stat_ref[...]
    lane = lax.broadcasted_iota(jnp.int32, stat.shape, 1)
    pick = lambda j: jnp.sum(jnp.where(lane == j, stat, 0.0), axis=1, keepdims=True)
    top = jnp.concatenate([pick(step * here + i) for i in range(here)], 0)
    total = jnp.concatenate([pick(heads + step * here + i) for i in range(here)], 0)
    return top, total, stacked(acc_ref)


def first_kernel(q_ref, own_k, own_v, line_ref, acc_ref, stat_ref, *, heads):
    tok = q_ref.shape[0]
    half = line_ref.shape[0] // 2
    q = stacked(q_ref)
    shape = (q.shape[0], tok)
    row = lax.rem(lax.broadcasted_iota(jnp.int32, shape, 0), tok)
    causal = lax.broadcasted_iota(jnp.int32, shape, 1) <= row
    parts = [
        (line_ref[:half], line_ref[half:], None),
        (own_k[...], own_v[...], causal),
    ]
    store_state(absorb(q, parts, None), acc_ref, stat_ref, heads)


def prompt_kernel(
    me, q_ref, whole_ref, acc_in, stat_in, acc_ref, stat_ref, keys, values, *, heads, half
):
    plane = whole_ref.shape[0]

    @pl.when(pl.program_id(0) == 0)
    def _():
        for i in range(1, plane):
            g = lax.rem(me[0] + i, plane)
            at = slice((i - 1) * half, i * half)
            keys[at] = whole_ref[g, :half]
            values[at] = whole_ref[g, half : 2 * half]

    parts = []
    for i in range(0, keys.shape[0], CHUNK):
        at = slice(i, min(i + CHUNK, keys.shape[0]))
        parts.append((keys[at], values[at], None))
    state = absorb(stacked(q_ref), parts, load_state(acc_in, stat_in, heads))
    store_state(state, acc_ref, stat_ref, heads)


def last_kernel(me, fork, lengths, q_ref, above_ref, acc_in, stat_in, o_ref, *, heads):
    tok = q_ref.shape[0]
    q = stacked(q_ref)
    seen = lax.broadcasted_iota(jnp.int32, (q.shape[0], tok), 1) < fork[me[1]]
    parts = [(above_ref[:tok], above_ref[tok:], seen)]
    _, total, acc = absorb(q, parts, load_state(acc_in, stat_in, heads))
    kept = lax.broadcasted_iota(jnp.int32, (tok, HEAD_DIM), 0) < lengths[me[1]]
    out = acc / total
    for i in range(q_ref.shape[1] // HEAD_DIM):
        at = slice(i * HEAD_DIM, (i + 1) * HEAD_DIM)
        o_ref[:, at] = jnp.where(kept, out[i * tok : (i + 1) * tok], 0.0).astype(o_ref.dtype)


def attention(kernel, name, q, tables, shared, state, outs, keys, per_step, scratch=()):
    tok, width = q.shape
    step = per_step * HEAD_DIM
    fixed = lambda a: pl.BlockSpec(a.shape, lambda h, *_: (0,) * a.ndim)
    moving = pl.BlockSpec((tok, step), lambda h, *_: (0, h))
    spec = lambda a: moving if a.shape[1] == width else fixed(a)
    return pl.pallas_call(
        kernel,
        name=name,
        out_shape=outs,
        grid_spec=pltpu.PrefetchScalarGridSpec(
            num_scalar_prefetch=len(tables),
            grid=(width // step,),
            in_specs=[moving] + [fixed(a) for a in shared] + [spec(a) for a in state],
            out_specs=jax.tree.map(spec, outs),
            scratch_shapes=scratch,
        ),
        compiler_params=pltpu.CompilerParams(vmem_limit_bytes=40 << 20),
        cost_estimate=pl.CostEstimate(
            flops=4 * tok * width * keys,
            transcendentals=tok * (width // HEAD_DIM) * keys,
            bytes_accessed=4 * tok * width + 4 * keys * HEAD_DIM,
        ),
    )(*tables, q, *shared, *state)


def choose_kernel(parent, whole_ref, o_ref, *, start):
    count, unit = o_ref.shape[0], o_ref.shape[1]
    each = count // whole_ref.shape[0]
    for b in range(count):
        p = jnp.maximum(parent[b], 0)
        at = pl.multiple_of(start + lax.rem(p, each) * unit, unit)
        o_ref[b] = whole_ref[p // each, pl.ds(at, unit)]


def exchange(a, axes):
    return lax.all_to_all(a, axes, split_axis=0, concat_axis=0, tiled=True)


def body(queries, branch_keys, branch_values, prompt_keys, prompt_values, parent, fork, lengths):
    tok, width = queries.shape
    heads = width // HEAD_DIM
    rows = prompt_keys.shape[0]
    ny, nh, nb = lax.axis_size("y"), lax.axis_size(HEAD), lax.axis_size(BRANCH)
    plane = lax.axis_size(PLANE)
    unit = 2 * tok // nb
    where = jnp.stack([lax.axis_index(PLANE), lax.axis_index(BRANCH)])

    split = lambda a: a.reshape(rows, nh, HEAD_DIM).transpose(1, 0, 2)
    mine = exchange(jnp.concatenate([split(prompt_keys), split(prompt_values)], 1), HEAD)
    half = nh * rows
    part = lambda a: a.reshape(half, HEAD_DIM)
    mine = jnp.concatenate([part(mine[:, :rows]), part(mine[:, rows:])], 0)
    own = jnp.concatenate([branch_keys, branch_values], 0)
    own = own.reshape(plane, ny, unit, HEAD_DIM).transpose(1, 0, 2, 3)
    own = own.reshape(ny, plane * unit, HEAD_DIM)
    spread = jnp.broadcast_to(mine[None], (ny,) + mine.shape)
    line = exchange(jnp.concatenate([spread, own], 1), "y")

    part = lambda a: a.reshape(ny * half, HEAD_DIM)
    prompt = jnp.concatenate([part(line[:, :half]), part(line[:, half : 2 * half])], 0)
    pieces = line[:, 2 * half :].reshape(ny, plane, unit, HEAD_DIM).transpose(1, 0, 2, 3)
    pieces = pieces.reshape(plane, ny * unit, HEAD_DIM)
    spread = jnp.broadcast_to(prompt[None], (plane,) + prompt.shape)
    whole = exchange(jnp.concatenate([spread, pieces], 1), PLANE)

    half = ny * half
    chosen = pl.pallas_call(
        functools.partial(choose_kernel, start=2 * half),
        name="choose",
        out_shape=jax.ShapeDtypeStruct((nb, unit, HEAD_DIM), jnp.bfloat16),
        in_specs=[
            pl.BlockSpec(memory_space=pltpu.SMEM),
            pl.BlockSpec(memory_space=pltpu.VMEM),
        ],
        out_specs=pl.BlockSpec(memory_space=pltpu.VMEM),
        compiler_params=pltpu.CompilerParams(vmem_limit_bytes=4 << 20),
    )(parent, whole)
    above = exchange(chosen, BRANCH).reshape(2 * tok, HEAD_DIM)

    state = (
        jax.ShapeDtypeStruct((tok, width), jnp.float32),
        jax.ShapeDtypeStruct((tok, HEAD_DIM), jnp.float32),
    )
    bound = lambda kernel, **more: functools.partial(kernel, heads=heads, **more)
    carried = attention(
        bound(first_kernel),
        "first",
        queries,
        (),
        (branch_keys, branch_values, prompt),
        (),
        state,
        tok + half,
        4,
    )
    rest = (plane - 1) * half
    carried = attention(
        bound(prompt_kernel, half=half),
        "rest",
        queries,
        (where,),
        (whole,),
        carried,
        state,
        rest,
        4,
        [pltpu.VMEM((rest, HEAD_DIM), jnp.bfloat16)] * 2,
    )
    out = jax.ShapeDtypeStruct((tok, width), jnp.bfloat16)
    return attention(
        bound(last_kernel),
        "last",
        queries,
        (where, fork, lengths),
        (above,),
        carried,
        out,
        tok,
        4,
    )


def solution(mesh):
    fine = Mesh(mesh.devices.reshape(4, 2, 8, 4, 2), BRANCH + HEAD)
    placed = (
        P(BRANCH, HEAD),
        P(BRANCH, HEAD),
        P(BRANCH, HEAD),
        P(BRANCH + HEAD, None),
        P(BRANCH + HEAD, None),
        P(),
        P(),
        P(),
    )
    return jax.shard_map(
        body, mesh=fine, in_specs=placed, out_specs=P(BRANCH, HEAD), check_vma=False
    )
```

time: 107 us -> 99.4 us (0.929)
  the two profiles are of different devices: /device:TPU:8 before, /device:TPU:1 now
where the time goes in v2:
time: 99.4 us; the launch traced here: 98.9 us
  Pallas kernels  25.2 us (25%)
  starting transfers between devices  25.1 us (25%)
  waiting for transfers between devices  23 us (23%)
  blocking collectives  18.3 us (18%)
  other arithmetic  3.7 us (4%)
  local copies, waits for them, and re-layouts  3.45 us (3%)
    all_to_all x3, starting transfers between devices, exchange(): return lax.all_to_all(a, axes, split_axis=0, concat_axis=0, tiled=True)  25.1 us
    pallas_call x3, Pallas kernels, attention(): pl.pallas_call(kernel, name=name, out_shape=outs, grid_spec=pltpu.Prefetc...  23.7 us
    all_to_all x3, waiting for transfers between devices, exchange(): return lax.all_to_all(a, axes, split_axis=0, concat_axis=0, tiled=True)  23 us
    all_to_all x1, blocking collectives, exchange(): return lax.all_to_all(a, axes, split_axis=0, concat_axis=0, tiled=True)  18.3 us
    unnamed x20, local copies, waits for them, and re-layouts  3.13 us
  transfers between devices with their start and end apart: 3, of which 2 were waited for; matrix products, arithmetic and copies ran while one was open for 1% of the time, Pallas kernels for 21%

profile of v2, /device:TPU:1, one launch (start us, length us, event | category | flops | bytes accessed | tf_op | source)
XLA Modules:
  0.0 98.9 jit_solution(14591448588056629009)
XLA Ops:
  0.0 1.4 %pad_maximum_fusion.4 = bf16[8,12,128]{2,1,0:T(8,128)(2,1)} fusion(bf16[8,6,128]{2,1,0:T(8,128)(2,1)} %bitcast.29, bf16[8,6,128]{2,1,0:T(8,128)(2,1)} %bitcast.30), kind=kLoop, calls=%fused_computation.7 | loop fusion | flops 49152 | bytes 49152 | tf_op jit(solution)/shard_map/concatenate | solution.py:175
  1.4 11.8 %all-to-all-start = ((bf16[8,12,128]{2,1,0:T(8,128)(2,1)}), bf16[8,12,128]{2,1,0:T(8,128)(2,1)S(1)}, u32[]{:S(2)}, u32[]{:S(2)}) async-start(bf16[8,12,128]{2,1,0:T(8,128)(2,1)} %pad_maximum_fusion.4), calls=%async_computation | async-start | bytes 65536 | tf_op jit(solution)/shard_map/all_to_all | solution.py:162
  13.2 0.9 pad_maximum_fusion.3
  14.1 6.4 %all-to-all-done = bf16[8,12,128]{2,1,0:T(8,128)(2,1)S(1)} async-done(((bf16[8,12,128]{2,1,0:T(8,128)(2,1)}), bf16[8,12,128]{2,1,0:T(8,128)(2,1)S(1)}, u32[]{:S(2)}, u32[]{:S(2)}) %all-to-all-start) | async-done | bytes 24608 | tf_op jit(solution)/shard_map/all_to_all | solution.py:162
  20.6 18.3 %all_to_all.20 = bf16[8,160,128]{2,1,0:T(8,128)(2,1)S(1)} all-to-all(bf16[8,160,128]{2,1,0:T(8,128)(2,1)S(1)} %pad_maximum_fusion.1), channel_id=1, replica_groups=mesh['x'=4,'zl'=2,'y'=8,'zh'=4,'c'=2] {'y'}, dimensions={0} | all-to-all | bytes 655360 | tf_op jit(solution)/shard_map/all_to_all | solution.py:162
  38.9 0.2 broadcast_in_dim.5
  39.1 1.3 %pad_maximum_fusion = bf16[8,832,128]{2,1,0:T(8,128)(2,1)} fusion(bf16[8,64,128]{2,1,0:T(8,128)(2,1)S(1)} %copy_bitcast_fusion, bf16[8,768,128]{2,1,0:T(8,128)(2,1)S(1)} %broadcast_in_dim.5), kind=kLoop, calls=%fused_computation | loop fusion | flops 3407872 | bytes 3407872 | tf_op jit(solution)/shard_map/concatenate | solution.py:190
  40.5 0.0 copy-start
  40.5 0.0 copy-start.1
  40.5 0.0 copy-start.2
  40.5 4.9 %all-to-all-start.2 = ((bf16[8,832,128]{2,1,0:T(8,128)(2,1)}), bf16[8,832,128]{2,1,0:T(8,128)(2,1)S(1)}, u32[]{:S(2)}, u32[]{:S(2)}) async-start(bf16[8,832,128]{2,1,0:T(8,128)(2,1)} %pad_maximum_fusion), calls=%async_computation.2 | async-start | bytes 3407872 | tf_op jit(solution)/shard_map/all_to_all | solution.py:162
  45.4 0.0 copy-start.5
  45.4 0.1 pad_add_fusion.me
  45.5 0.0 copy-done
  45.5 0.0 copy-done.1
  45.5 0.0 copy-done.2
  45.5 2.3 %first.1 = (f32[256,1024]{1,0:T(8,128)S(1)}, f32[256,128]{1,0:T(8,128)S(1)}) custom-call(bf16[256,1024]{1,0:T(8,128)(2,1)S(1)} %copy-done, bf16[256,128]{1,0:T(8,128)(2,1)S(1)} %copy-done.2, bf16[256,128]{1,0:T(8,128)(2,1)S(1)} %copy-done.1, bf16[768,128]{1,0:T(8,128)(2,1)S(1)} %pad_maximum_fusion.2.line_ref), custom_call_target="tpu_custom_call" | custom-call | flops 671088640 | bytes 1376256 | tf_op jit(solution)/shard_map/first/pallas_call | solution.py:132
  47.8 0.0 copy-start.6
  47.8 1.0 copy-done.6
  48.7 0.0 copy-start.8
  48.7 16.6 %all-to-all-done.2.whole_ref = bf16[8,832,128]{2,1,0:T(8,128)(2,1)S(1)} async-done(((bf16[8,832,128]{2,1,0:T(8,128)(2,1)}), bf16[8,832,128]{2,1,0:T(8,128)(2,1)S(1)}, u32[]{:S(2)}, u32[]{:S(2)}) %all-to-all-start.2) | async-done | bytes 1703968 | tf_op jit(solution)/shard_map/all_to_all | solution.py:162
  65.4 0.0 copy-done.5
  65.4 1.5 %choose.1 = bf16[64,8,128]{2,1,0:T(8,128)(2,1)} custom-call(s32[64]{0:T(128)S(1)} %copy-done.5, bf16[8,832,128]{2,1,0:T(8,128)(2,1)S(1)} %all-to-all-done.2.whole_ref), custom_call_target="tpu_custom_call" | custom-call | tf_op jit(solution)/shard_map/choose/pallas_call | solution.py:193
  66.9 0.0 copy-done.8
  66.9 8.4 %all-to-all-start.3 = ((bf16[64,8,128]{2,1,0:T(8,128)(2,1)}), bf16[64,8,128]{2,1,0:T(8,128)(2,1)S(1)}, u32[]{:S(2)}, u32[]{:S(2)}) async-start(bf16[64,8,128]{2,1,0:T(8,128)(2,1)} %choose.1), calls=%async_computation.3 | async-start | bytes 262144 | tf_op jit(solution)/shard_map/all_to_all | solution.py:162
  75.3 0.0 copy-start.7
  75.3 1.2 %copy-done.7 = f32[256,1024]{1,0:T(8,128)S(1)} copy-done((f32[256,1024]{1,0:T(8,128)S(1)}, f32[256,1024]{1,0:T(8,128)}, u32[]{:S(2)}) %copy-start.7) | copy-done | bytes 1048600
  76.5 0.0 copy-start.9
  76.5 0.9 copy-done.9
  77.4 0.0 copy-start.3
  77.4 0.0 copy-start.4
  77.4 18.1 %rest.1 = (f32[256,1024]{1,0:T(8,128)S(1)}, f32[256,128]{1,0:T(8,128)S(1)}) custom-call(s32[2]{0:T(128)S(1)} %pad_add_fusion.me, bf16[256,1024]{1,0:T(8,128)(2,1)S(1)} %copy-done, bf16[8,832,128]{2,1,0:T(8,128)(2,1)S(1)} %all-to-all-done.2.whole_ref, f32[256,1024]{1,0:T(8,128)S(1)} %copy-done.7, f32[256,128]{1,0:T(8,128)S(1)} %copy-done.9), custom_call_target="tpu_custom_call" | custom-call | flops 2818572288 | bytes 2424832 | tf_op jit(solution)/shard_map/rest/pallas_call | solution.py:132
  95.5 0.0 all-to-all-done.3
  95.5 0.0 copy-done.3
  95.5 0.0 copy-done.4
  95.5 3.3 %last.1 = bf16[256,1024]{1,0:T(8,128)(2,1)} custom-call(s32[2]{0:T(128)S(1)} %pad_add_fusion.me, s32[64]{0:T(128)S(1)} %copy-done.3, s32[64]{0:T(128)S(1)} %copy-done.4, bf16[256,1024]{1,0:T(8,128)(2,1)S(1)} %copy-done, bf16[512,128]{1,0:T(8,128)(2,1)S(1)} %bitcast.24, f32[256,1024]{1,0:T(8,128)S(1)} %get-tuple-element.11.acc_in, ...), custom_call_target="tpu_custom_call" | custom-call | flops 268435456 | bytes 1179648 | tf_op jit(solution)/shard_map/last/pallas_call | solution.py:132
  (10 shorter events, 0.2 us)
Async XLA Ops:
  1.4 19.1 %all-to-all-start = ((bf16[8,12,128]{2,1,0:T(8,128)(2,1)}), bf16[8,12,128]{2,1,0:T(8,128)(2,1)S(1)}, u32[]{:S(2)}, u32[]{:S(2)}) async-start(bf16[8,12,128]{2,1,0:T(8,128)(2,1)} %pad_maximum_fusion.4), calls=%async_computation | async-start | bytes 65536 | tf_op jit(solution)/shard_map/all_to_all | solution.py:162
  40.5 5.0 %copy-start = (bf16[256,1024]{1,0:T(8,128)(2,1)S(1)}, bf16[256,1024]{1,0:T(8,128)(2,1)}, u32[]{:S(2)}) copy-start(bf16[256,1024]{1,0:T(8,128)(2,1)} %q_ref.5) | copy-start | bytes 1572868
  40.5 5.0 %copy-start.1 = (bf16[256,128]{1,0:T(8,128)(2,1)S(1)}, bf16[256,128]{1,0:T(8,128)(2,1)}, u32[]{:S(2)}) copy-start(bf16[256,128]{1,0:T(8,128)(2,1)} %own_v.1) | copy-start | bytes 196612
  40.5 5.0 %copy-start.2 = (bf16[256,128]{1,0:T(8,128)(2,1)S(1)}, bf16[256,128]{1,0:T(8,128)(2,1)}, u32[]{:S(2)}) copy-start(bf16[256,128]{1,0:T(8,128)(2,1)} %own_k.1) | copy-start | bytes 196612
  40.5 24.9 %all-to-all-start.2 = ((bf16[8,832,128]{2,1,0:T(8,128)(2,1)}), bf16[8,832,128]{2,1,0:T(8,128)(2,1)S(1)}, u32[]{:S(2)}, u32[]{:S(2)}) async-start(bf16[8,832,128]{2,1,0:T(8,128)(2,1)} %pad_maximum_fusion), calls=%async_computation.2 | async-start | bytes 3407872 | tf_op jit(solution)/shard_map/all_to_all | solution.py:162
  45.4 20.0 %copy-start.5 = (s32[64]{0:T(128)S(1)}, s32[64]{0:T(128)}, u32[]{:S(2)}) copy-start(s32[64]{0:T(128)} %parent.1) | copy-start | bytes 772
  47.8 1.0 copy-start.6
  48.7 18.1 %copy-start.8 = (f32[256,128]{1,0:T(8,128)}, f32[256,128]{1,0:T(8,128)S(1)}, u32[]{:S(2)}) copy-start(f32[256,128]{1,0:T(8,128)S(1)} %get-tuple-element.10.stat_in) | copy-start | bytes 393220
  66.9 28.6 %all-to-all-start.3 = ((bf16[64,8,128]{2,1,0:T(8,128)(2,1)}), bf16[64,8,128]{2,1,0:T(8,128)(2,1)S(1)}, u32[]{:S(2)}, u32[]{:S(2)}) async-start(bf16[64,8,128]{2,1,0:T(8,128)(2,1)} %choose.1), calls=%async_computation.3 | async-start | bytes 262144 | tf_op jit(solution)/shard_map/all_to_all | solution.py:162
  75.3 1.2 %copy-start.7 = (f32[256,1024]{1,0:T(8,128)S(1)}, f32[256,1024]{1,0:T(8,128)}, u32[]{:S(2)}) copy-start(f32[256,1024]{1,0:T(8,128)} %copy-done.6) | copy-start | bytes 3145732
  76.5 0.9 copy-start.9
  77.4 18.1 %copy-start.3 = (s32[64]{0:T(128)S(1)}, s32[64]{0:T(128)}, u32[]{:S(2)}) copy-start(s32[64]{0:T(128)} %fork.1) | copy-start | bytes 772
  77.4 18.1 %copy-start.4 = (s32[64]{0:T(128)S(1)}, s32[64]{0:T(128)}, u32[]{:S(2)}) copy-start(s32[64]{0:T(128)} %lengths.1) | copy-start | bytes 772

commit v3 on v2

v3 whole, which is shorter than its diff:
```python
import functools
import math

import jax
import jax.numpy as jnp
from jax import lax
from jax.experimental import pallas as pl
from jax.experimental.pallas import tpu as pltpu
from jax.sharding import Mesh, PartitionSpec as P


HEAD_DIM = 128
SCALE2 = math.log2(math.e) / math.sqrt(HEAD_DIM)
NEG = -1e30
CHUNK = 512
BRANCH = ("x", "zl", "y")
HEAD = ("zh", "c")
CONTRACT_LAST = (((1,), (1,)), ((), ()))
CONTRACT_MID = (((1,), (0,)), ((), ()))


def absorb(q, parts, state):
    for k, v, mask in parts:
        s = lax.dot_general(q, k, CONTRACT_LAST, preferred_element_type=jnp.float32)
        if mask is not None:
            s = jnp.where(mask, s, NEG)
        top = jnp.max(s, axis=1, keepdims=True)
        if state is not None:
            top = jnp.maximum(state[0], top)
        w = jnp.exp2((s - top) * SCALE2).astype(jnp.bfloat16)
        both = lax.dot_general(
            w,
            jnp.concatenate([v, jnp.ones_like(v)], 1),
            CONTRACT_MID,
            preferred_element_type=jnp.float32,
        )
        acc, total = both[:, :HEAD_DIM], both[:, HEAD_DIM:]
        if state is not None:
            fade = jnp.exp2((state[0] - top) * SCALE2)
            total += state[1] * fade
            acc += state[2] * fade
        state = (top, total, acc)
    return state


def stacked(ref):
    return jnp.concatenate(
        [ref[:, i : i + HEAD_DIM] for i in range(0, ref.shape[1], HEAD_DIM)], 0
    )


def store_state(state, acc_ref, stat_ref, heads):
    top, total, acc = state
    tok = acc_ref.shape[0]
    here = acc_ref.shape[1] // HEAD_DIM
    step = pl.program_id(0)
    lane = lax.broadcasted_iota(jnp.int32, (tok, HEAD_DIM), 1)
    stat = stat_ref[...]
    for i in range(here):
        at = slice(i * tok, (i + 1) * tok)
        acc_ref[:, i * HEAD_DIM : (i + 1) * HEAD_DIM] = acc[at]
        stat = jnp.where(lane == step * here + i, top[at], stat)
        stat = jnp.where(lane == heads + step * here + i, total[at], stat)
    stat_ref[...] = stat


def load_state(acc_ref, stat_ref, heads):
    here = acc_ref.shape[1] // HEAD_DIM
    step = pl.program_id(0)
    stat = stat_ref[...]
    lane = lax.broadcasted_iota(jnp.int32, stat.shape, 1)
    pick = lambda j: jnp.sum(jnp.where(lane == j, stat, 0.0), axis=1, keepdims=True)
    top = jnp.concatenate([pick(step * here + i) for i in range(here)], 0)
    total = jnp.concatenate([pick(heads + step * here + i) for i in range(here)], 0)
    return top, total, stacked(acc_ref)


def prompt_kernel(q_ref, *refs, heads):
    blocks, (own_k, own_v, acc_ref, stat_ref, keys, values) = refs[:-6], refs[-6:]
    tok = q_ref.shape[0]

    @pl.when(pl.program_id(0) == 0)
    def _():
        start = 0
        for block in blocks:
            half = block.shape[1] // 2
            for i in range(block.shape[0]):
                keys[start : start + half] = block[i, :half]
                values[start : start + half] = block[i, half:]
                start += half

    q = stacked(q_ref)
    shape = (q.shape[0], tok)
    row = lax.rem(lax.broadcasted_iota(jnp.int32, shape, 0), tok)
    causal = lax.broadcasted_iota(jnp.int32, shape, 1) <= row
    parts = [
        (keys[i : i + CHUNK], values[i : i + CHUNK], None) for i in range(0, keys.shape[0], CHUNK)
    ]
    parts.append((own_k[...], own_v[...], causal))
    store_state(absorb(q, parts, None), acc_ref, stat_ref, heads)


def last_kernel(me, fork, lengths, q_ref, above_ref, acc_in, stat_in, o_ref, *, heads):
    tok = q_ref.shape[0]
    q = stacked(q_ref)
    seen = lax.broadcasted_iota(jnp.int32, (q.shape[0], tok), 1) < fork[me[0]]
    parts = [(above_ref[:tok], above_ref[tok:], seen)]
    _, total, acc = absorb(q, parts, load_state(acc_in, stat_in, heads))
    kept = lax.broadcasted_iota(jnp.int32, (tok, HEAD_DIM), 0) < lengths[me[0]]
    out = acc / total
    for i in range(q_ref.shape[1] // HEAD_DIM):
        at = slice(i * HEAD_DIM, (i + 1) * HEAD_DIM)
        o_ref[:, at] = jnp.where(kept, out[i * tok : (i + 1) * tok], 0.0).astype(o_ref.dtype)


def attention(kernel, q, tables, shared, state, outs, keys, per_step, scratch=()):
    tok, width = q.shape
    step = per_step * HEAD_DIM
    fixed = lambda a: pl.BlockSpec(a.shape, lambda h, *_: (0,) * a.ndim)
    moving = pl.BlockSpec((tok, step), lambda h, *_: (0, h))
    spec = lambda a: moving if a.shape[1] == width else fixed(a)
    return pl.pallas_call(
        kernel,
        out_shape=outs,
        grid_spec=pltpu.PrefetchScalarGridSpec(
            num_scalar_prefetch=len(tables),
            grid=(width // step,),
            in_specs=[moving] + [fixed(a) for a in shared] + [spec(a) for a in state],
            out_specs=jax.tree.map(spec, outs),
            scratch_shapes=scratch,
        ),
        compiler_params=pltpu.CompilerParams(vmem_limit_bytes=40 << 20),
        cost_estimate=pl.CostEstimate(
            flops=4 * tok * width * keys,
            transcendentals=tok * (width // HEAD_DIM) * keys,
            bytes_accessed=4 * tok * width + 4 * keys * HEAD_DIM,
        ),
    )(*tables, q, *shared, *state)


def choose_kernel(parent, pieces_ref, o_ref):
    for b in range(o_ref.shape[0]):
        o_ref[b] = pieces_ref[jnp.maximum(parent[b], 0)]


def exchange(a, axes):
    return lax.all_to_all(a, axes, split_axis=0, concat_axis=0, tiled=True)


def shifted(a, axis, step):
    n = lax.axis_size(axis)
    return lax.ppermute(a, axis, [(i, (i + step) % n) for i in range(n)])


def body(queries, branch_keys, branch_values, prompt_keys, prompt_values, parent, fork, lengths):
    tok, width = queries.shape
    heads = width // HEAD_DIM
    rows = prompt_keys.shape[0]
    ny, nh, nb = lax.axis_size("y"), lax.axis_size(HEAD), lax.axis_size(BRANCH)
    unit = 2 * tok // nb
    me = lax.axis_index(BRANCH).reshape(1)

    split = lambda a: a.reshape(rows, nh, HEAD_DIM).transpose(1, 0, 2)
    mine = jnp.concatenate([split(prompt_keys), split(prompt_values)], 1)
    spread = jnp.broadcast_to(mine[None], (ny,) + mine.shape)
    line = exchange(spread.reshape(ny * nh, 2 * rows, HEAD_DIM), ("y",) + HEAD)
    half = ny * nh * rows
    part = lambda a: a.reshape(half, HEAD_DIM)
    line = jnp.concatenate([part(line[:, :rows]), part(line[:, rows:])], 0)
    other = shifted(line, "zl", 1)
    block = jnp.stack([line, other])
    blocks = [block] + [shifted(block, "x", step) for step in range(1, lax.axis_size("x"))]

    own = jnp.concatenate([branch_keys, branch_values], 0)
    pieces = exchange(own.reshape(nb, unit, HEAD_DIM), BRANCH)
    chosen = pl.pallas_call(
        choose_kernel,
        name="choose",
        out_shape=jax.ShapeDtypeStruct((nb, unit, HEAD_DIM), jnp.bfloat16),
        in_specs=[
            pl.BlockSpec(memory_space=pltpu.SMEM),
            pl.BlockSpec(memory_space=pltpu.VMEM),
        ],
        out_specs=pl.BlockSpec(memory_space=pltpu.VMEM),
        compiler_params=pltpu.CompilerParams(vmem_limit_bytes=4 << 20),
    )(parent, pieces)
    above = exchange(chosen, BRANCH).reshape(2 * tok, HEAD_DIM)

    state = (
        jax.ShapeDtypeStruct((tok, width), jnp.float32),
        jax.ShapeDtypeStruct((tok, HEAD_DIM), jnp.float32),
    )
    bound = lambda kernel: functools.partial(kernel, heads=heads)
    keys = len(blocks) * 2 * half
    carried = attention(
        bound(prompt_kernel),
        queries,
        (),
        (*blocks, branch_keys, branch_values),
        (),
        state,
        keys + tok,
        4,
        [pltpu.VMEM((keys, HEAD_DIM), jnp.bfloat16)] * 2,
    )
    out = jax.ShapeDtypeStruct((tok, width), jnp.bfloat16)
    return attention(
        bound(last_kernel), queries, (me, fork, lengths), (above,), carried, out, tok, 8
    )


def solution(mesh):
    fine = Mesh(mesh.devices.reshape(4, 2, 8, 4, 2), BRANCH + HEAD)
    placed = (
        P(BRANCH, HEAD),
        P(BRANCH, HEAD),
        P(BRANCH, HEAD),
        P(BRANCH + HEAD, None),
        P(BRANCH + HEAD, None),
        P(),
        P(),
        P(),
    )

    return jax.shard_map(
        body, mesh=fine, in_specs=placed, out_specs=P(BRANCH, HEAD), check_vma=False
    )
```

time: 99.4 us -> 90.8 us (0.913)
  the two profiles are of different devices: /device:TPU:1 before, /device:TPU:8 now
where the time goes in v3:
time: 90.8 us; the launch traced here: 90.3 us
  blocking collectives  31 us (34%)
  starting transfers between devices  25.8 us (28%)
  waiting for transfers between devices  17.9 us (20%)
  Pallas kernels  13.1 us (14%)
  local copies, waits for them, and re-layouts  1.64 us (2%)
    all_to_all x1, blocking collectives, exchange(): return lax.all_to_all(a, axes, split_axis=0, concat_axis=0, tiled=True)  31 us
    ppermute x4, starting transfers between devices, shifted(): return lax.ppermute(a, axis, [(i, (i + step) % n) for i in range(n)])  14.9 us
    all_to_all x2, waiting for transfers between devices, exchange(): return lax.all_to_all(a, axes, split_axis=0, concat_axis=0, tiled=True)  12 us
    pallas_call x2, Pallas kernels, attention(): pl.pallas_call(kernel, out_shape=outs, grid_spec=pltpu.PrefetchScalarGrid...  11.8 us
    all_to_all x2, starting transfers between devices, exchange(): return lax.all_to_all(a, axes, split_axis=0, concat_axis=0, tiled=True)  10.9 us
    ppermute x4, waiting for transfers between devices, shifted(): return lax.ppermute(a, axis, [(i, (i + step) % n) for i in range(n)])  5.86 us
  transfers between devices with their start and end apart: 6, of which 3 were waited for; matrix products, arithmetic and copies ran while one was open for 1% of the time, Pallas kernels for 11%

profile of v3, /device:TPU:8, one launch (start us, length us, event | category | flops | bytes accessed | tf_op | source)
XLA Modules:
  0.0 90.3 jit_solution(13500488940543652869)
XLA Ops:
  0.0 0.7 bitcast_bitcast_fusion
  0.8 31.0 %all_to_all.15 = bf16[64,12,128]{2,1,0:T(8,128)(2,1)S(1)} all-to-all(bf16[64,12,128]{2,1,0:T(8,128)(2,1)S(1)} %bitcast.18), channel_id=1, replica_groups=mesh['x'=4,'zl'=2,'y'=8,'zh'=4,'c'=2] {'y','zh','c'}, dimensions={0} | all-to-all | bytes 393216 | tf_op jit(solution)/shard_map/all_to_all | solution.py:147
  31.8 0.1 fusion
  32.0 3.4 %collective-permute-start = (bf16[768,128]{1,0:T(8,128)(2,1)S(1)}, bf16[768,128]{1,0:T(8,128)(2,1)S(1)}, u32[]{:S(2)}, u32[]{:S(2)}) collective-permute-start(bf16[768,128]{1,0:T(8,128)(2,1)S(1)} %constant_dynamic-update-slice_fusion), channel_id=1, source_target_pairs={{0,64},{64,0},{1,65},{65,1},{2,66},{66,2},{3,67},{67,3},{4,68},{68... | collective-permute-start | bytes 589832 | tf_op jit(solution)/shard_map/ppermute | solution.py:152
  35.4 5.9 %collective-permute-done = bf16[768,128]{1,0:T(8,128)(2,1)S(1)} collective-permute-done((bf16[768,128]{1,0:T(8,128)(2,1)S(1)}, bf16[768,128]{1,0:T(8,128)(2,1)S(1)}, u32[]{:S(2)}, u32[]{:S(2)}) %collective-permute-start) | collective-permute-done | bytes 196640 | tf_op jit(solution)/shard_map/ppermute | solution.py:152
  41.2 0.0 copy-start.1
  41.2 0.0 copy-start.2
  41.3 0.0 copy-start
  41.3 3.5 %collective-permute-start.1 = (bf16[2,768,128]{2,1,0:T(8,128)(2,1)S(1)}, bf16[2,768,128]{2,1,0:T(8,128)(2,1)S(1)}, u32[]{:S(2)}, u32[]{:S(2)}) collective-permute-start(bf16[2,768,128]{2,1,0:T(8,128)(2,1)S(1)} %pad_maximum_fusion.refs_0_), channel_id=1, source_target_pairs={{0,128},{128,256},{256,384},{384,0},{1,129},{129,257},{257,385},{3... | collective-permute-start | bytes 1179656 | tf_op jit(solution)/shard_map/ppermute | solution.py:152
  44.8 4.6 %collective-permute-start.2 = (bf16[2,768,128]{2,1,0:T(8,128)(2,1)S(1)}, bf16[2,768,128]{2,1,0:T(8,128)(2,1)S(1)}, u32[]{:S(2)}, u32[]{:S(2)}) collective-permute-start(bf16[2,768,128]{2,1,0:T(8,128)(2,1)S(1)} %pad_maximum_fusion.refs_0_), channel_id=1, source_target_pairs={{0,256},{128,384},{256,0},{384,128},{1,257},{129,385},{257,1},{385... | collective-permute-start | bytes 1179656 | tf_op jit(solution)/shard_map/ppermute | solution.py:152
  49.5 3.3 %collective-permute-start.3 = (bf16[2,768,128]{2,1,0:T(8,128)(2,1)S(1)}, bf16[2,768,128]{2,1,0:T(8,128)(2,1)S(1)}, u32[]{:S(2)}, u32[]{:S(2)}) collective-permute-start(bf16[2,768,128]{2,1,0:T(8,128)(2,1)S(1)} %pad_maximum_fusion.refs_0_), channel_id=1, source_target_pairs={{0,384},{128,0},{256,128},{384,256},{1,385},{129,1},{257,129},{385... | collective-permute-start | bytes 1179656 | tf_op jit(solution)/shard_map/ppermute | solution.py:152
  52.8 0.0 copy-done.1
  52.8 0.0 copy-done.2
  52.8 0.7 maximum_bitcast_fusion
  53.5 5.0 %all-to-all-start = ((bf16[64,8,128]{2,1,0:T(8,128)(2,1)}), bf16[64,8,128]{2,1,0:T(8,128)(2,1)S(1)}, u32[]{:S(2)}, u32[]{:S(2)}) async-start(bf16[64,8,128]{2,1,0:T(8,128)(2,1)} %maximum_bitcast_fusion), calls=%async_computation | async-start | bytes 262144 | tf_op jit(solution)/shard_map/all_to_all | solution.py:147
  58.6 0.0 copy-start.3
  58.6 10.4 %all-to-all-done.pieces_ref = bf16[64,8,128]{2,1,0:T(8,128)(2,1)S(1)} async-done(((bf16[64,8,128]{2,1,0:T(8,128)(2,1)}), bf16[64,8,128]{2,1,0:T(8,128)(2,1)S(1)}, u32[]{:S(2)}, u32[]{:S(2)}) %all-to-all-start) | async-done | bytes 131104 | tf_op jit(solution)/shard_map/all_to_all | solution.py:147
  68.9 0.0 copy-done.3
  68.9 1.3 %choose.1 = bf16[64,8,128]{2,1,0:T(8,128)(2,1)} custom-call(s32[64]{0:T(128)S(1)} %copy-done.3, bf16[64,8,128]{2,1,0:T(8,128)(2,1)S(1)} %all-to-all-done.pieces_ref), custom_call_target="tpu_custom_call" | custom-call | tf_op jit(solution)/shard_map/choose/pallas_call | solution.py:176
  70.2 5.8 %all-to-all-start.1 = ((bf16[64,8,128]{2,1,0:T(8,128)(2,1)}), bf16[64,8,128]{2,1,0:T(8,128)(2,1)S(1)}, u32[]{:S(2)}, u32[]{:S(2)}) async-start(bf16[64,8,128]{2,1,0:T(8,128)(2,1)} %choose.1), calls=%async_computation.1 | async-start | bytes 262144 | tf_op jit(solution)/shard_map/all_to_all | solution.py:147
  76.1 0.0 collective-permute-done.1.refs_1_
  76.1 0.0 collective-permute-done.2.refs_2_
  76.1 0.0 collective-permute-done.3.refs_3_
  76.1 0.0 copy-done
  76.1 8.7 %shard_map.82 = (f32[256,1024]{1,0:T(8,128)S(1)}, f32[256,128]{1,0:T(8,128)S(1)}) custom-call(bf16[256,1024]{1,0:T(8,128)(2,1)S(1)} %copy-done, bf16[2,768,128]{2,1,0:T(8,128)(2,1)S(1)} %pad_maximum_fusion.refs_0_, bf16[2,768,128]{2,1,0:T(8,128)(2,1)S(1)} %collective-permute-done.1.refs_1_, bf16[2,768,128]{2,1,0:T(8,128)(2,1)S(1)} %collective-permute-done.2.refs_2_, ...), custom_call_target="tpu_custom_call" | custom-call | flops 3489660928 | bytes 2752512 | tf_op jit(solution)/shard_map/pallas_call | solution.py:122
  84.8 1.6 %all-to-all-done.1 = bf16[64,8,128]{2,1,0:T(8,128)(2,1)S(1)} async-done(((bf16[64,8,128]{2,1,0:T(8,128)(2,1)}), bf16[64,8,128]{2,1,0:T(8,128)(2,1)S(1)}, u32[]{:S(2)}, u32[]{:S(2)}) %all-to-all-start.1) | async-done | bytes 131104 | tf_op jit(solution)/shard_map/all_to_all | solution.py:147
  86.5 0.0 copy-start.4
  86.5 0.0 copy-start.5
  86.5 0.7 copy-done.4
  87.1 0.0 copy-done.5
  87.2 3.1 %shard_map.83 = bf16[256,1024]{1,0:T(8,128)(2,1)} custom-call(s32[1]{0:T(128)} %bitcast.me, s32[64]{0:T(128)S(1)} %copy-done.4, s32[64]{0:T(128)S(1)} %copy-done.5, bf16[256,1024]{1,0:T(8,128)(2,1)S(1)} %copy-done, bf16[512,128]{1,0:T(8,128)(2,1)S(1)} %bitcast.17, f32[256,1024]{1,0:T(8,128)S(1)} %get-tuple-element.7.acc_in, ...), custom_call_target="tpu_custom_call" | custom-call | flops 268435456 | bytes 1179648 | tf_op jit(solution)/shard_map/pallas_call | solution.py:122
  (8 shorter events, 0.2 us)
Async XLA Ops:
  32.0 9.2 %collective-permute-start = (bf16[768,128]{1,0:T(8,128)(2,1)S(1)}, bf16[768,128]{1,0:T(8,128)(2,1)S(1)}, u32[]{:S(2)}, u32[]{:S(2)}) collective-permute-start(bf16[768,128]{1,0:T(8,128)(2,1)S(1)} %constant_dynamic-update-slice_fusion), channel_id=1, source_target_pairs={{0,64},{64,0},{1,65},{65,1},{2,66},{66,2},{3,67},{67,3},{4,68},{68... | collective-permute-start | bytes 589832 | tf_op jit(solution)/shard_map/ppermute | solution.py:152
  41.2 11.6 %copy-start.1 = (bf16[256,128]{1,0:T(8,128)(2,1)S(1)}, bf16[256,128]{1,0:T(8,128)(2,1)}, u32[]{:S(2)}) copy-start(bf16[256,128]{1,0:T(8,128)(2,1)} %refs_5_.1) | copy-start | bytes 196612
  41.2 11.6 %copy-start.2 = (bf16[256,128]{1,0:T(8,128)(2,1)S(1)}, bf16[256,128]{1,0:T(8,128)(2,1)}, u32[]{:S(2)}) copy-start(bf16[256,128]{1,0:T(8,128)(2,1)} %refs_4_.1) | copy-start | bytes 196612
  41.3 34.8 %copy-start = (bf16[256,1024]{1,0:T(8,128)(2,1)S(1)}, bf16[256,1024]{1,0:T(8,128)(2,1)}, u32[]{:S(2)}) copy-start(bf16[256,1024]{1,0:T(8,128)(2,1)} %q_ref.3) | copy-start | bytes 1572868
  41.3 34.8 %collective-permute-start.1 = (bf16[2,768,128]{2,1,0:T(8,128)(2,1)S(1)}, bf16[2,768,128]{2,1,0:T(8,128)(2,1)S(1)}, u32[]{:S(2)}, u32[]{:S(2)}) collective-permute-start(bf16[2,768,128]{2,1,0:T(8,128)(2,1)S(1)} %pad_maximum_fusion.refs_0_), channel_id=1, source_target_pairs={{0,128},{128,256},{256,384},{384,0},{1,129},{129,257},{257,385},{3... | collective-permute-start | bytes 1179656 | tf_op jit(solution)/shard_map/ppermute | solution.py:152
  44.8 31.3 %collective-permute-start.2 = (bf16[2,768,128]{2,1,0:T(8,128)(2,1)S(1)}, bf16[2,768,128]{2,1,0:T(8,128)(2,1)S(1)}, u32[]{:S(2)}, u32[]{:S(2)}) collective-permute-start(bf16[2,768,128]{2,1,0:T(8,128)(2,1)S(1)} %pad_maximum_fusion.refs_0_), channel_id=1, source_target_pairs={{0,256},{128,384},{256,0},{384,128},{1,257},{129,385},{257,1},{385... | collective-permute-start | bytes 1179656 | tf_op jit(solution)/shard_map/ppermute | solution.py:152
  49.5 26.6 %collective-permute-start.3 = (bf16[2,768,128]{2,1,0:T(8,128)(2,1)S(1)}, bf16[2,768,128]{2,1,0:T(8,128)(2,1)S(1)}, u32[]{:S(2)}, u32[]{:S(2)}) collective-permute-start(bf16[2,768,128]{2,1,0:T(8,128)(2,1)S(1)} %pad_maximum_fusion.refs_0_), channel_id=1, source_target_pairs={{0,384},{128,0},{256,128},{384,256},{1,385},{129,1},{257,129},{385... | collective-permute-start | bytes 1179656 | tf_op jit(solution)/shard_map/ppermute | solution.py:152
  53.5 15.4 %all-to-all-start = ((bf16[64,8,128]{2,1,0:T(8,128)(2,1)}), bf16[64,8,128]{2,1,0:T(8,128)(2,1)S(1)}, u32[]{:S(2)}, u32[]{:S(2)}) async-start(bf16[64,8,128]{2,1,0:T(8,128)(2,1)} %maximum_bitcast_fusion), calls=%async_computation | async-start | bytes 262144 | tf_op jit(solution)/shard_map/all_to_all | solution.py:147
  58.6 10.4 %copy-start.3 = (s32[64]{0:T(128)S(1)}, s32[64]{0:T(128)}, u32[]{:S(2)}) copy-start(s32[64]{0:T(128)} %parent.1) | copy-start | bytes 772
  70.2 16.3 %all-to-all-start.1 = ((bf16[64,8,128]{2,1,0:T(8,128)(2,1)}), bf16[64,8,128]{2,1,0:T(8,128)(2,1)S(1)}, u32[]{:S(2)}, u32[]{:S(2)}) async-start(bf16[64,8,128]{2,1,0:T(8,128)(2,1)} %choose.1), calls=%async_computation.1 | async-start | bytes 262144 | tf_op jit(solution)/shard_map/all_to_all | solution.py:147
  86.5 0.7 copy-start.4
  86.5 0.7 copy-start.5

commit v4 on v3

v4 whole, which is shorter than its diff:
```python
import math

import jax
import jax.numpy as jnp
from jax import lax
from jax.experimental import pallas as pl
from jax.experimental.pallas import tpu as pltpu
from jax.sharding import Mesh, PartitionSpec as P


HEAD_DIM = 128
SCALE2 = math.log2(math.e) / math.sqrt(HEAD_DIM)
NEG = -1e30
CHUNK = 512
GROUP = 4
BRANCH = ("x", "zl", "y")
HEAD = ("zh", "c")
CONTRACT_LAST = (((1,), (1,)), ((), ()))
CONTRACT_MID = (((1,), (0,)), ((), ()))


def absorb(q, parts, state):
    for k, v, mask in parts:
        s = lax.dot_general(q, k, CONTRACT_LAST, preferred_element_type=jnp.float32)
        if mask is not None:
            s = jnp.where(mask, s, NEG)
        top = jnp.max(s, axis=1, keepdims=True)
        if state is not None:
            top = jnp.maximum(state[0], top)
        w = jnp.exp2((s - top) * SCALE2).astype(jnp.bfloat16)
        both = lax.dot_general(
            w,
            jnp.concatenate([v, jnp.ones_like(v)], 1),
            CONTRACT_MID,
            preferred_element_type=jnp.float32,
        )
        acc, total = both[:, :HEAD_DIM], both[:, HEAD_DIM:]
        if state is not None:
            fade = jnp.exp2((state[0] - top) * SCALE2)
            total += state[1] * fade
            acc += state[2] * fade
        state = (top, total, acc)
    return state


def lanes(first, count):
    return pl.ds(pl.multiple_of(first * HEAD_DIM, HEAD_DIM), count * HEAD_DIM)


def stacked(ref, step):
    return jnp.concatenate([ref[:, lanes(step * GROUP + i, 1)] for i in range(GROUP)], 0)


def split_rows(a):
    tok = a.shape[0] // GROUP
    return [a[i * tok : (i + 1) * tok] for i in range(GROUP)]


def store_state(state, acc_ref, stat_ref, step):
    top, total, acc = (split_rows(a) for a in state)
    heads = acc_ref.shape[1] // HEAD_DIM
    stat = stat_ref[...]
    lane = lax.broadcasted_iota(jnp.int32, stat.shape, 1)
    for i in range(GROUP):
        head = step * GROUP + i
        acc_ref[:, lanes(head, 1)] = acc[i]
        stat = jnp.where(lane == head, top[i], stat)
        stat = jnp.where(lane == heads + head, total[i], stat)
    stat_ref[...] = stat


def load_state(acc_ref, stat_ref, step):
    heads = acc_ref.shape[1] // HEAD_DIM
    stat = stat_ref[...]
    lane = lax.broadcasted_iota(jnp.int32, stat.shape, 1)
    pick = lambda j: jnp.sum(jnp.where(lane == j, stat, 0.0), axis=1, keepdims=True)
    top = jnp.concatenate([pick(step * GROUP + i) for i in range(GROUP)], 0)
    total = jnp.concatenate([pick(heads + step * GROUP + i) for i in range(GROUP)], 0)
    return top, total, stacked(acc_ref, step)


def gather_rows(blocks, keys, values):
    start = 0
    for block in blocks:
        half = block.shape[1] // 2
        for i in range(block.shape[0]):
            keys[start : start + half] = block[i, :half]
            values[start : start + half] = block[i, half:]
            start += half


def chunks(keys, values):
    ends = range(0, keys.shape[0], CHUNK)
    return [(keys[i : i + CHUNK], values[i : i + CHUNK], None) for i in ends]


def most_kernel(q_ref, *refs):
    blocks, (own_k, own_v, acc_ref, stat_ref, keys, values) = refs[:-6], refs[-6:]
    tok, width = q_ref.shape
    gather_rows(blocks, keys, values)
    stat_ref[...] = jnp.zeros_like(stat_ref)

    @pl.loop(0, width // HEAD_DIM // GROUP)
    def _(step):
        q = stacked(q_ref, step)
        shape = (q.shape[0], tok)
        row = lax.rem(lax.broadcasted_iota(jnp.int32, shape, 0), tok)
        causal = lax.broadcasted_iota(jnp.int32, shape, 1) <= row
        parts = chunks(keys, values) + [(own_k[...], own_v[...], causal)]
        store_state(absorb(q, parts, None), acc_ref, stat_ref, step)


def last_kernel(me, tables, q_ref, far_ref, above_ref, acc_in, stat_in, o_ref, keys, values):
    tok, width = q_ref.shape
    count = tables.shape[0] // 3
    fork, live = tables[count + me[0]], tables[2 * count + me[0]]
    gather_rows([far_ref], keys, values)

    @pl.loop(0, width // HEAD_DIM // GROUP)
    def _(step):
        q = stacked(q_ref, step)
        seen = lax.broadcasted_iota(jnp.int32, (q.shape[0], tok), 1) < fork
        parts = chunks(keys, values) + [(above_ref[:tok], above_ref[tok:], seen)]
        _, total, acc = absorb(q, parts, load_state(acc_in, stat_in, step))
        kept = lax.broadcasted_iota(jnp.int32, (tok, HEAD_DIM), 0) < live
        for i, out in enumerate(split_rows(acc / total)):
            at = lanes(step * GROUP + i, 1)
            o_ref[:, at] = jnp.where(kept, out, 0.0).astype(o_ref.dtype)


def attention(kernel, tables, arrays, outs, keys, scratch_rows):
    tok, width = arrays[0].shape
    vmem = pl.BlockSpec(memory_space=pltpu.VMEM)
    smem = pl.BlockSpec(memory_space=pltpu.SMEM)
    return pl.pallas_call(
        kernel,
        out_shape=outs,
        in_specs=[smem] * len(tables) + [vmem] * len(arrays),
        out_specs=jax.tree.map(lambda _: vmem, outs),
        scratch_shapes=[pltpu.VMEM((scratch_rows, HEAD_DIM), jnp.bfloat16)] * 2,
        compiler_params=pltpu.CompilerParams(vmem_limit_bytes=32 << 20),
        cost_estimate=pl.CostEstimate(
            flops=4 * tok * width * keys,
            transcendentals=tok * (width // HEAD_DIM) * keys,
            bytes_accessed=4 * tok * width + 4 * keys * HEAD_DIM,
        ),
    )(*tables, *arrays)


def choose_kernel(parent, pieces_ref, o_ref):
    for b in range(o_ref.shape[0]):
        o_ref[b] = pieces_ref[jnp.maximum(parent[b], 0)]


def exchange(a, axes):
    return lax.all_to_all(a, axes, split_axis=0, concat_axis=0, tiled=True)


def shifted(a, axis, step):
    n = lax.axis_size(axis)
    return lax.ppermute(a, axis, [(i, (i + step) % n) for i in range(n)])


def body(queries, branch_keys, branch_values, prompt_keys, prompt_values, parent, fork, lengths):
    tok, width = queries.shape
    rows = prompt_keys.shape[0]
    ny, nz, nc, nb = (lax.axis_size(a) for a in ("y", "zh", "c", BRANCH))
    unit = 2 * tok // nb
    me = lax.axis_index(BRANCH).reshape(1)
    first_core = lax.axis_index("c") == 0
    tables = jnp.concatenate([parent, fork, lengths])

    both = jnp.stack([prompt_keys, prompt_values]).reshape(2, rows, nz, nc, HEAD_DIM)
    kept = jnp.where(first_core, both[:, :, :, 0], both[:, :, :, 1])
    given = jnp.where(first_core, both[:, :, :, 1], both[:, :, :, 0])
    taken = shifted(given, "c", 1)
    mine = jnp.concatenate([kept, taken], 1).transpose(2, 0, 1, 3)
    mine = mine.reshape(nz, 2 * nc * rows, HEAD_DIM)
    spread = jnp.broadcast_to(mine[None], (ny,) + mine.shape)
    line = exchange(spread.reshape(ny * nz, 2 * nc * rows, HEAD_DIM), ("y", "zh"))
    half = ny * nz * nc * rows
    part = lambda a: a.reshape(half, HEAD_DIM)
    line = jnp.concatenate([part(line[:, : nc * rows]), part(line[:, nc * rows :])], 0)
    other = shifted(line, "zl", 1)
    block = jnp.stack([line, other])
    near = [block, shifted(block, "x", 1), shifted(block, "x", -1)]
    far = shifted(block, "x", 2)

    own = jnp.concatenate([branch_keys, branch_values], 0).reshape(nb, unit, HEAD_DIM)
    pieces = exchange(own, BRANCH)
    chosen = pl.pallas_call(
        choose_kernel,
        name="choose",
        out_shape=jax.ShapeDtypeStruct((nb, unit, HEAD_DIM), jnp.bfloat16),
        in_specs=[
            pl.BlockSpec(memory_space=pltpu.SMEM),
            pl.BlockSpec(memory_space=pltpu.VMEM),
        ],
        out_specs=pl.BlockSpec(memory_space=pltpu.VMEM),
        compiler_params=pltpu.CompilerParams(vmem_limit_bytes=4 << 20),
    )(tables, pieces)
    above = exchange(chosen, BRANCH).reshape(2 * tok, HEAD_DIM)

    state = (
        jax.ShapeDtypeStruct((tok, width), jnp.float32),
        jax.ShapeDtypeStruct((tok, HEAD_DIM), jnp.float32),
    )
    keys = len(near) * 2 * half
    carried = attention(
        most_kernel, (), (queries, *near, branch_keys, branch_values), state, keys + tok, keys
    )
    out = jax.ShapeDtypeStruct((tok, width), jnp.bfloat16)
    arrays = (queries, far, above, *carried)
    return attention(last_kernel, (me, tables), arrays, out, 2 * half + tok, 2 * half)


def solution(mesh):
    fine = Mesh(mesh.devices.reshape(4, 2, 8, 4, 2), BRANCH + HEAD)
    placed = (
        P(BRANCH, HEAD),
        P(BRANCH, HEAD),
        P(BRANCH, HEAD),
        P(BRANCH + HEAD, None),
        P(BRANCH + HEAD, None),
        P(),
        P(),
        P(),
    )

    return jax.shard_map(
        body, mesh=fine, in_specs=placed, out_specs=P(BRANCH, HEAD), check_vma=False
    )
```

time: 90.8 us -> 90.9 us (level)
  waiting for transfers between devices: 17.9 us -> 14.3 us
  starting transfers between devices: 25.8 us -> 29.1 us
  Pallas kernels: 13.1 us -> 14.6 us
  blocking collectives: 31 us -> 29.6 us
    all_to_all x2, waiting for transfers between devices: 12 us -> 8.9 us  [exchange(): return lax.all_to_all(a, axes, split_axis=0, concat_axis=0, tiled=True)]
    ppermute x4 -> x5, starting transfers between devices: 14.9 us -> 17.4 us  [shifted(): return lax.ppermute(a, axis, [(i, (i + step) % n) for i in range(n)])]
    pallas_call x2, Pallas kernels: 11.8 us -> 13.3 us  [attention(): pl.pallas_call(kernel, out_shape=outs, in_specs=[smem] * len(tables) + [v...]
    all_to_all x1, blocking collectives: 31 us -> 29.6 us  [exchange(): return lax.all_to_all(a, axes, split_axis=0, concat_axis=0, tiled=True)]
    ppermute x4 -> x5, waiting for transfers between devices: 5.86 us -> 5.35 us  [shifted(): return lax.ppermute(a, axis, [(i, (i + step) % n) for i in range(n)])]
  transfers between devices with their start and end apart: 6 -> 7, of which waited for: 3 -> 4; matrix products, arithmetic and copies ran while one was open for 1% -> 1% of each run, Pallas kernels for 11% -> 9%
where the time goes in v4:
time: 90.9 us; the launch traced here: 90.4 us
  blocking collectives  29.6 us (33%)
  starting transfers between devices  29.1 us (32%)
  Pallas kernels  14.6 us (16%)
  waiting for transfers between devices  14.3 us (16%)
  local copies, waits for them, and re-layouts  1.68 us (2%)
    all_to_all x1, blocking collectives, exchange(): return lax.all_to_all(a, axes, split_axis=0, concat_axis=0, tiled=True)  29.6 us
    ppermute x5, starting transfers between devices, shifted(): return lax.ppermute(a, axis, [(i, (i + step) % n) for i in range(n)])  17.4 us
    pallas_call x2, Pallas kernels, attention(): pl.pallas_call(kernel, out_shape=outs, in_specs=[smem] * len(tables) + [v...  13.3 us
    all_to_all x2, starting transfers between devices, exchange(): return lax.all_to_all(a, axes, split_axis=0, concat_axis=0, tiled=True)  11.7 us
    all_to_all x2, waiting for transfers between devices, exchange(): return lax.all_to_all(a, axes, split_axis=0, concat_axis=0, tiled=True)  8.9 us
    ppermute x5, waiting for transfers between devices, shifted(): return lax.ppermute(a, axis, [(i, (i + step) % n) for i in range(n)])  5.35 us
  transfers between devices with their start and end apart: 7, of which 4 were waited for; matrix products, arithmetic and copies ran while one was open for 1% of the time, Pallas kernels for 9%

profile of v4, /device:TPU:8, one launch (start us, length us, event | category | flops | bytes accessed | tf_op | source)
XLA Modules:
  0.0 90.4 jit_solution(16824087270319603069)
XLA Ops:
  0.0 0.7 stack.18
  0.7 0.0 copy-start.3
  0.8 0.7 copy-done.3
  1.5 0.1 broadcast_select_fusion.1
  1.6 1.9 %collective-permute-start = (bf16[2,6,4,128]{3,2,1,0:T(4,128)(2,1)S(1)}, bf16[2,6,4,128]{3,2,1,0:T(4,128)(2,1)S(1)}, u32[]{:S(2)}, u32[]{:S(2)}) collective-permute-start(bf16[2,6,4,128]{3,2,1,0:T(4,128)(2,1)S(1)} %bitcast.22), channel_id=1, source_target_pairs={{0,1},{1,0},{2,3},{3,2},{4,5},{5,4},{6,7},{7,6},{8,9},{9,8},{10,11... | collective-permute-start | bytes 36872 | tf_op jit(solution)/shard_map/ppermute | solution.py:161
  3.5 1.1 %collective-permute-done = bf16[2,6,4,128]{3,2,1,0:T(4,128)(2,1)S(1)} collective-permute-done((bf16[2,6,4,128]{3,2,1,0:T(4,128)(2,1)S(1)}, bf16[2,6,4,128]{3,2,1,0:T(4,128)(2,1)S(1)}, u32[]{:S(2)}, u32[]{:S(2)}) %collective-permute-start) | collective-permute-done | bytes 12320 | tf_op jit(solution)/shard_map/ppermute | solution.py:161
  4.7 29.6 %all_to_all.15 = bf16[32,24,128]{2,1,0:T(8,128)(2,1)S(1)} all-to-all(bf16[32,24,128]{2,1,0:T(8,128)(2,1)S(1)} %bitcast.17), channel_id=1, replica_groups=mesh['x'=4,'zl'=2,'y'=8,'zh'=4,'c'=2] {'y','zh'}, dimensions={0} | all-to-all | bytes 393216 | tf_op jit(solution)/shard_map/all_to_all | solution.py:156
  34.5 3.3 %collective-permute-start.1 = (bf16[768,128]{1,0:T(8,128)(2,1)S(1)}, bf16[768,128]{1,0:T(8,128)(2,1)S(1)}, u32[]{:S(2)}, u32[]{:S(2)}) collective-permute-start(bf16[768,128]{1,0:T(8,128)(2,1)S(1)} %constant_dynamic-update-slice_fusion.2), channel_id=1, source_target_pairs={{0,64},{64,0},{1,65},{65,1},{2,66},{66,2},{3,67},{67,3},{4,68},{68... | collective-permute-start | bytes 589832 | tf_op jit(solution)/shard_map/ppermute | solution.py:161
  37.9 4.2 %collective-permute-done.1 = bf16[768,128]{1,0:T(8,128)(2,1)S(1)} collective-permute-done((bf16[768,128]{1,0:T(8,128)(2,1)S(1)}, bf16[768,128]{1,0:T(8,128)(2,1)S(1)}, u32[]{:S(2)}, u32[]{:S(2)}) %collective-permute-start.1) | collective-permute-done | bytes 196640 | tf_op jit(solution)/shard_map/ppermute | solution.py:161
  42.1 0.0 copy-start
  42.1 0.0 copy-start.1
  42.1 0.0 copy-start.4
  42.1 0.0 copy-start.5
  42.1 0.0 copy-start.6
  42.1 0.0 copy-start.2
  42.1 3.5 %collective-permute-start.3 = (bf16[2,768,128]{2,1,0:T(8,128)(2,1)S(1)}, bf16[2,768,128]{2,1,0:T(8,128)(2,1)S(1)}, u32[]{:S(2)}, u32[]{:S(2)}) collective-permute-start(bf16[2,768,128]{2,1,0:T(8,128)(2,1)S(1)} %pad_maximum_fusion.refs_0_), channel_id=1, source_target_pairs={{0,128},{128,256},{256,384},{384,0},{1,129},{129,257},{257,385},{3... | collective-permute-start | bytes 1179656 | tf_op jit(solution)/shard_map/ppermute | solution.py:161
  45.7 3.7 %collective-permute-start.4 = (bf16[2,768,128]{2,1,0:T(8,128)(2,1)S(1)}, bf16[2,768,128]{2,1,0:T(8,128)(2,1)S(1)}, u32[]{:S(2)}, u32[]{:S(2)}) collective-permute-start(bf16[2,768,128]{2,1,0:T(8,128)(2,1)S(1)} %pad_maximum_fusion.refs_0_), channel_id=1, source_target_pairs={{0,384},{128,0},{256,128},{384,256},{1,385},{129,1},{257,129},{385... | collective-permute-start | bytes 1179656 | tf_op jit(solution)/shard_map/ppermute | solution.py:161
  49.3 0.0 copy-done
  49.4 0.0 copy-done.1
  49.4 0.7 maximum_bitcast_fusion
  50.0 6.4 %all-to-all-start.1 = ((bf16[64,8,128]{2,1,0:T(8,128)(2,1)}), bf16[64,8,128]{2,1,0:T(8,128)(2,1)S(1)}, u32[]{:S(2)}, u32[]{:S(2)}) async-start(bf16[64,8,128]{2,1,0:T(8,128)(2,1)} %maximum_bitcast_fusion), calls=%async_computation.1 | async-start | bytes 262144 | tf_op jit(solution)/shard_map/all_to_all | solution.py:156
  56.5 5.0 %collective-permute-start.2 = (bf16[2,768,128]{2,1,0:T(8,128)(2,1)S(1)}, bf16[2,768,128]{2,1,0:T(8,128)(2,1)S(1)}, u32[]{:S(2)}, u32[]{:S(2)}) collective-permute-start(bf16[2,768,128]{2,1,0:T(8,128)(2,1)S(1)} %pad_maximum_fusion.refs_0_), channel_id=1, source_target_pairs={{0,256},{128,384},{256,0},{384,128},{1,257},{129,385},{257,1},{385... | collective-permute-start | bytes 1179656 | tf_op jit(solution)/shard_map/ppermute | solution.py:161
  61.5 0.0 copy-done.4
  61.5 0.0 copy-done.5
  61.5 0.0 copy-done.6
  61.5 0.1 pad_add_fusion.parent.tables
  61.6 5.3 %all-to-all-done.1.pieces_ref = bf16[64,8,128]{2,1,0:T(8,128)(2,1)S(1)} async-done(((bf16[64,8,128]{2,1,0:T(8,128)(2,1)}), bf16[64,8,128]{2,1,0:T(8,128)(2,1)S(1)}, u32[]{:S(2)}, u32[]{:S(2)}) %all-to-all-start.1) | async-done | bytes 131104 | tf_op jit(solution)/shard_map/all_to_all | solution.py:156
  66.9 1.3 %choose.1 = bf16[64,8,128]{2,1,0:T(8,128)(2,1)} custom-call(s32[192]{0:T(256)S(1)} %pad_add_fusion.parent.tables, bf16[64,8,128]{2,1,0:T(8,128)(2,1)S(1)} %all-to-all-done.1.pieces_ref), custom_call_target="tpu_custom_call" | custom-call | tf_op jit(solution)/shard_map/choose/pallas_call | solution.py:191
  68.2 5.2 %all-to-all-start.2 = ((bf16[64,8,128]{2,1,0:T(8,128)(2,1)}), bf16[64,8,128]{2,1,0:T(8,128)(2,1)S(1)}, u32[]{:S(2)}, u32[]{:S(2)}) async-start(bf16[64,8,128]{2,1,0:T(8,128)(2,1)} %choose.1), calls=%async_computation.2 | async-start | bytes 262144 | tf_op jit(solution)/shard_map/all_to_all | solution.py:156
  73.4 0.0 collective-permute-done.3.refs_1_
  73.5 0.0 collective-permute-done.4.refs_2_
  73.5 0.0 copy-done.2
  73.5 6.9 %shard_map.82 = (f32[256,1024]{1,0:T(8,128)S(1)}, f32[256,128]{1,0:T(8,128)S(1)}) custom-call(bf16[256,1024]{1,0:T(8,128)(2,1)S(1)} %copy-done.2, bf16[2,768,128]{2,1,0:T(8,128)(2,1)S(1)} %pad_maximum_fusion.refs_0_, bf16[2,768,128]{2,1,0:T(8,128)(2,1)S(1)} %collective-permute-done.3.refs_1_, bf16[2,768,128]{2,1,0:T(8,128)(2,1)S(1)} %collective-permute-done.4.refs_2_, ...), custom_call_target="tpu_custom_call" | custom-call | flops 2684354560 | bytes 2359296 | tf_op jit(solution)/shard_map/pallas_call | solution.py:135
  80.4 3.6 %all-to-all-done.2 = bf16[64,8,128]{2,1,0:T(8,128)(2,1)S(1)} async-done(((bf16[64,8,128]{2,1,0:T(8,128)(2,1)}), bf16[64,8,128]{2,1,0:T(8,128)(2,1)S(1)}, u32[]{:S(2)}, u32[]{:S(2)}) %all-to-all-start.2) | async-done | bytes 131104 | tf_op jit(solution)/shard_map/all_to_all | solution.py:156
  84.0 0.0 collective-permute-done.2.far_ref
  84.0 6.4 %shard_map.83 = bf16[256,1024]{1,0:T(8,128)(2,1)} custom-call(s32[1]{0:T(128)} %bitcast.me, s32[192]{0:T(256)S(1)} %pad_add_fusion.parent.tables, bf16[256,1024]{1,0:T(8,128)(2,1)S(1)} %copy-done.2, bf16[2,768,128]{2,1,0:T(8,128)(2,1)S(1)} %collective-permute-done.2.far_ref, bf16[512,128]{1,0:T(8,128)(2,1)S(1)} %bitcast.16, ...), custom_call_target="tpu_custom_call" | custom-call | flops 1073741824 | bytes 1572864 | tf_op jit(solution)/shard_map/pallas_call | solution.py:135
  (14 shorter events, 0.3 us)
Async XLA Ops:
  0.7 0.7 copy-start.3
  1.6 3.1 %collective-permute-start = (bf16[2,6,4,128]{3,2,1,0:T(4,128)(2,1)S(1)}, bf16[2,6,4,128]{3,2,1,0:T(4,128)(2,1)S(1)}, u32[]{:S(2)}, u32[]{:S(2)}) collective-permute-start(bf16[2,6,4,128]{3,2,1,0:T(4,128)(2,1)S(1)} %bitcast.22), channel_id=1, source_target_pairs={{0,1},{1,0},{2,3},{3,2},{4,5},{5,4},{6,7},{7,6},{8,9},{9,8},{10,11... | collective-permute-start | bytes 36872 | tf_op jit(solution)/shard_map/ppermute | solution.py:161
  34.5 7.6 %collective-permute-start.1 = (bf16[768,128]{1,0:T(8,128)(2,1)S(1)}, bf16[768,128]{1,0:T(8,128)(2,1)S(1)}, u32[]{:S(2)}, u32[]{:S(2)}) collective-permute-start(bf16[768,128]{1,0:T(8,128)(2,1)S(1)} %constant_dynamic-update-slice_fusion.2), channel_id=1, source_target_pairs={{0,64},{64,0},{1,65},{65,1},{2,66},{66,2},{3,67},{67,3},{4,68},{68... | collective-permute-start | bytes 589832 | tf_op jit(solution)/shard_map/ppermute | solution.py:161
  42.1 7.3 %copy-start = (bf16[256,128]{1,0:T(8,128)(2,1)S(1)}, bf16[256,128]{1,0:T(8,128)(2,1)}, u32[]{:S(2)}) copy-start(bf16[256,128]{1,0:T(8,128)(2,1)} %refs_4_.1) | copy-start | bytes 196612
  42.1 7.3 %copy-start.1 = (bf16[256,128]{1,0:T(8,128)(2,1)S(1)}, bf16[256,128]{1,0:T(8,128)(2,1)}, u32[]{:S(2)}) copy-start(bf16[256,128]{1,0:T(8,128)(2,1)} %refs_3_.1) | copy-start | bytes 196612
  42.1 19.4 %copy-start.4 = (s32[64]{0:T(128)S(1)}, s32[64]{0:T(128)}, u32[]{:S(2)}) copy-start(s32[64]{0:T(128)} %param.15) | copy-start | bytes 772
  42.1 19.4 %copy-start.5 = (s32[64]{0:T(128)S(1)}, s32[64]{0:T(128)}, u32[]{:S(2)}) copy-start(s32[64]{0:T(128)} %param.14) | copy-start | bytes 772
  42.1 19.4 %copy-start.6 = (s32[64]{0:T(128)S(1)}, s32[64]{0:T(128)}, u32[]{:S(2)}) copy-start(s32[64]{0:T(128)} %param.13) | copy-start | bytes 772
  42.1 31.3 %copy-start.2 = (bf16[256,1024]{1,0:T(8,128)(2,1)S(1)}, bf16[256,1024]{1,0:T(8,128)(2,1)}, u32[]{:S(2)}) copy-start(bf16[256,1024]{1,0:T(8,128)(2,1)} %q_ref.3) | copy-start | bytes 1572868
  42.1 31.3 %collective-permute-start.3 = (bf16[2,768,128]{2,1,0:T(8,128)(2,1)S(1)}, bf16[2,768,128]{2,1,0:T(8,128)(2,1)S(1)}, u32[]{:S(2)}, u32[]{:S(2)}) collective-permute-start(bf16[2,768,128]{2,1,0:T(8,128)(2,1)S(1)} %pad_maximum_fusion.refs_0_), channel_id=1, source_target_pairs={{0,128},{128,256},{256,384},{384,0},{1,129},{129,257},{257,385},{3... | collective-permute-start | bytes 1179656 | tf_op jit(solution)/shard_map/ppermute | solution.py:161
  45.7 27.8 %collective-permute-start.4 = (bf16[2,768,128]{2,1,0:T(8,128)(2,1)S(1)}, bf16[2,768,128]{2,1,0:T(8,128)(2,1)S(1)}, u32[]{:S(2)}, u32[]{:S(2)}) collective-permute-start(bf16[2,768,128]{2,1,0:T(8,128)(2,1)S(1)} %pad_maximum_fusion.refs_0_), channel_id=1, source_target_pairs={{0,384},{128,0},{256,128},{384,256},{1,385},{129,1},{257,129},{385... | collective-permute-start | bytes 1179656 | tf_op jit(solution)/shard_map/ppermute | solution.py:161
  50.0 16.9 %all-to-all-start.1 = ((bf16[64,8,128]{2,1,0:T(8,128)(2,1)}), bf16[64,8,128]{2,1,0:T(8,128)(2,1)S(1)}, u32[]{:S(2)}, u32[]{:S(2)}) async-start(bf16[64,8,128]{2,1,0:T(8,128)(2,1)} %maximum_bitcast_fusion), calls=%async_computation.1 | async-start | bytes 262144 | tf_op jit(solution)/shard_map/all_to_all | solution.py:156
  56.5 27.5 %collective-permute-start.2 = (bf16[2,768,128]{2,1,0:T(8,128)(2,1)S(1)}, bf16[2,768,128]{2,1,0:T(8,128)(2,1)S(1)}, u32[]{:S(2)}, u32[]{:S(2)}) collective-permute-start(bf16[2,768,128]{2,1,0:T(8,128)(2,1)S(1)} %pad_maximum_fusion.refs_0_), channel_id=1, source_target_pairs={{0,256},{128,384},{256,0},{384,128},{1,257},{129,385},{257,1},{385... | collective-permute-start | bytes 1179656 | tf_op jit(solution)/shard_map/ppermute | solution.py:161
  68.2 15.7 %all-to-all-start.2 = ((bf16[64,8,128]{2,1,0:T(8,128)(2,1)}), bf16[64,8,128]{2,1,0:T(8,128)(2,1)S(1)}, u32[]{:S(2)}, u32[]{:S(2)}) async-start(bf16[64,8,128]{2,1,0:T(8,128)(2,1)} %choose.1), calls=%async_computation.2 | async-start | bytes 262144 | tf_op jit(solution)/shard_map/all_to_all | solution.py:156

commit v5 on v3

--- a/solution.py
+++ b/solution.py
@@ -100,13 +100,15 @@
     store_state(absorb(q, parts, None), acc_ref, stat_ref, heads)
 
 
-def last_kernel(me, fork, lengths, q_ref, above_ref, acc_in, stat_in, o_ref, *, heads):
+def last_kernel(me, tables, q_ref, above_ref, acc_in, stat_in, o_ref, *, heads):
     tok = q_ref.shape[0]
+    count = tables.shape[0] // 3
+    fork, live = tables[count + me[0]], tables[2 * count + me[0]]
     q = stacked(q_ref)
-    seen = lax.broadcasted_iota(jnp.int32, (q.shape[0], tok), 1) < fork[me[0]]
+    seen = lax.broadcasted_iota(jnp.int32, (q.shape[0], tok), 1) < fork
     parts = [(above_ref[:tok], above_ref[tok:], seen)]
     _, total, acc = absorb(q, parts, load_state(acc_in, stat_in, heads))
-    kept = lax.broadcasted_iota(jnp.int32, (tok, HEAD_DIM), 0) < lengths[me[0]]
+    kept = lax.broadcasted_iota(jnp.int32, (tok, HEAD_DIM), 0) < live
     out = acc / total
     for i in range(q_ref.shape[1] // HEAD_DIM):
         at = slice(i * HEAD_DIM, (i + 1) * HEAD_DIM)
@@ -159,6 +161,7 @@
     ny, nh, nb = lax.axis_size("y"), lax.axis_size(HEAD), lax.axis_size(BRANCH)
     unit = 2 * tok // nb
     me = lax.axis_index(BRANCH).reshape(1)
+    tables = jnp.concatenate([parent, fork, lengths])
 
     split = lambda a: a.reshape(rows, nh, HEAD_DIM).transpose(1, 0, 2)
     mine = jnp.concatenate([split(prompt_keys), split(prompt_values)], 1)
@@ -171,8 +174,8 @@
     block = jnp.stack([line, other])
     blocks = [block] + [shifted(block, "x", step) for step in range(1, lax.axis_size("x"))]
 
-    own = jnp.concatenate([branch_keys, branch_values], 0)
-    pieces = exchange(own.reshape(nb, unit, HEAD_DIM), BRANCH)
+    own = jnp.concatenate([branch_keys, branch_values], 0).reshape(nb, unit, HEAD_DIM)
+    pieces = exchange(own, BRANCH)
     chosen = pl.pallas_call(
         choose_kernel,
         name="choose",
@@ -183,7 +186,7 @@
         ],
         out_specs=pl.BlockSpec(memory_space=pltpu.VMEM),
         compiler_params=pltpu.CompilerParams(vmem_limit_bytes=4 << 20),
-    )(parent, pieces)
+    )(tables, pieces)
     above = exchange(chosen, BRANCH).reshape(2 * tok, HEAD_DIM)
 
     state = (
@@ -204,9 +207,7 @@
         [pltpu.VMEM((keys, HEAD_DIM), jnp.bfloat16)] * 2,
     )
     out = jax.ShapeDtypeStruct((tok, width), jnp.bfloat16)
-    return attention(
-        bound(last_kernel), queries, (me, fork, lengths), (above,), carried, out, tok, 8
-    )
+    return attention(bound(last_kernel), queries, (me, tables), (above,), carried, out, tok, 8)
 
 
 def solution(mesh):

time: 90.8 us -> 90.2 us (level)
  no operation moved by 1% of the time
where the time goes in v5:
time: 90.2 us; the launch traced here: 89.6 us
  blocking collectives  31 us (34%)
  starting transfers between devices  25.8 us (29%)
  waiting for transfers between devices  17.1 us (19%)
  Pallas kernels  13.1 us (15%)
  local copies, waits for them, and re-layouts  1.63 us (2%)
    all_to_all x1, blocking collectives, exchange(): return lax.all_to_all(a, axes, split_axis=0, concat_axis=0, tiled=True)  31 us
    ppermute x4, starting transfers between devices, shifted(): return lax.ppermute(a, axis, [(i, (i + step) % n) for i in range(n)])  14.9 us
    pallas_call x2, Pallas kernels, attention(): pl.pallas_call(kernel, out_shape=outs, grid_spec=pltpu.PrefetchScalarGrid...  11.8 us
    all_to_all x2, waiting for transfers between devices, exchange(): return lax.all_to_all(a, axes, split_axis=0, concat_axis=0, tiled=True)  11.3 us
    all_to_all x2, starting transfers between devices, exchange(): return lax.all_to_all(a, axes, split_axis=0, concat_axis=0, tiled=True)  10.9 us
    ppermute x4, waiting for transfers between devices, shifted(): return lax.ppermute(a, axis, [(i, (i + step) % n) for i in range(n)])  5.86 us
  transfers between devices with their start and end apart: 6, of which 3 were waited for; matrix products, arithmetic and copies ran while one was open for 1% of the time, Pallas kernels for 11%

profile of v5, /device:TPU:8, one launch (start us, length us, event | category | flops | bytes accessed | tf_op | source)
XLA Modules:
  0.0 89.6 jit_solution(2249102553193405609)
XLA Ops:
  0.0 0.7 bitcast_bitcast_fusion
  0.8 31.0 %all_to_all.15 = bf16[64,12,128]{2,1,0:T(8,128)(2,1)S(1)} all-to-all(bf16[64,12,128]{2,1,0:T(8,128)(2,1)S(1)} %bitcast.18), channel_id=1, replica_groups=mesh['x'=4,'zl'=2,'y'=8,'zh'=4,'c'=2] {'y','zh','c'}, dimensions={0} | all-to-all | bytes 393216 | tf_op jit(solution)/shard_map/all_to_all | solution.py:149
  31.8 0.1 fusion
  32.0 3.4 %collective-permute-start = (bf16[768,128]{1,0:T(8,128)(2,1)S(1)}, bf16[768,128]{1,0:T(8,128)(2,1)S(1)}, u32[]{:S(2)}, u32[]{:S(2)}) collective-permute-start(bf16[768,128]{1,0:T(8,128)(2,1)S(1)} %constant_dynamic-update-slice_fusion), channel_id=1, source_target_pairs={{0,64},{64,0},{1,65},{65,1},{2,66},{66,2},{3,67},{67,3},{4,68},{68... | collective-permute-start | bytes 589832 | tf_op jit(solution)/shard_map/ppermute | solution.py:154
  35.4 5.9 %collective-permute-done = bf16[768,128]{1,0:T(8,128)(2,1)S(1)} collective-permute-done((bf16[768,128]{1,0:T(8,128)(2,1)S(1)}, bf16[768,128]{1,0:T(8,128)(2,1)S(1)}, u32[]{:S(2)}, u32[]{:S(2)}) %collective-permute-start) | collective-permute-done | bytes 196640 | tf_op jit(solution)/shard_map/ppermute | solution.py:154
  41.2 0.0 copy-start.1
  41.2 0.0 copy-start.2
  41.3 0.0 copy-start
  41.3 3.5 %collective-permute-start.1 = (bf16[2,768,128]{2,1,0:T(8,128)(2,1)S(1)}, bf16[2,768,128]{2,1,0:T(8,128)(2,1)S(1)}, u32[]{:S(2)}, u32[]{:S(2)}) collective-permute-start(bf16[2,768,128]{2,1,0:T(8,128)(2,1)S(1)} %pad_maximum_fusion.refs_0_), channel_id=1, source_target_pairs={{0,128},{128,256},{256,384},{384,0},{1,129},{129,257},{257,385},{3... | collective-permute-start | bytes 1179656 | tf_op jit(solution)/shard_map/ppermute | solution.py:154
  44.8 4.6 %collective-permute-start.2 = (bf16[2,768,128]{2,1,0:T(8,128)(2,1)S(1)}, bf16[2,768,128]{2,1,0:T(8,128)(2,1)S(1)}, u32[]{:S(2)}, u32[]{:S(2)}) collective-permute-start(bf16[2,768,128]{2,1,0:T(8,128)(2,1)S(1)} %pad_maximum_fusion.refs_0_), channel_id=1, source_target_pairs={{0,256},{128,384},{256,0},{384,128},{1,257},{129,385},{257,1},{385... | collective-permute-start | bytes 1179656 | tf_op jit(solution)/shard_map/ppermute | solution.py:154
  49.5 3.3 %collective-permute-start.3 = (bf16[2,768,128]{2,1,0:T(8,128)(2,1)S(1)}, bf16[2,768,128]{2,1,0:T(8,128)(2,1)S(1)}, u32[]{:S(2)}, u32[]{:S(2)}) collective-permute-start(bf16[2,768,128]{2,1,0:T(8,128)(2,1)S(1)} %pad_maximum_fusion.refs_0_), channel_id=1, source_target_pairs={{0,384},{128,0},{256,128},{384,256},{1,385},{129,1},{257,129},{385... | collective-permute-start | bytes 1179656 | tf_op jit(solution)/shard_map/ppermute | solution.py:154
  52.8 0.0 copy-done.1
  52.8 0.0 copy-done.2
  52.8 0.7 maximum_bitcast_fusion
  53.5 5.0 %all-to-all-start = ((bf16[64,8,128]{2,1,0:T(8,128)(2,1)}), bf16[64,8,128]{2,1,0:T(8,128)(2,1)S(1)}, u32[]{:S(2)}, u32[]{:S(2)}) async-start(bf16[64,8,128]{2,1,0:T(8,128)(2,1)} %maximum_bitcast_fusion), calls=%async_computation | async-start | bytes 262144 | tf_op jit(solution)/shard_map/all_to_all | solution.py:149
  58.6 0.0 copy-start.3
  58.6 0.0 copy-start.4
  58.6 0.0 copy-start.5
  58.6 0.6 copy-done.3
  59.2 0.0 copy-done.4
  59.2 0.0 copy-done.5
  59.2 0.1 pad_add_fusion.parent.tables
  59.3 9.6 %all-to-all-done.pieces_ref = bf16[64,8,128]{2,1,0:T(8,128)(2,1)S(1)} async-done(((bf16[64,8,128]{2,1,0:T(8,128)(2,1)}), bf16[64,8,128]{2,1,0:T(8,128)(2,1)S(1)}, u32[]{:S(2)}, u32[]{:S(2)}) %all-to-all-start) | async-done | bytes 131104 | tf_op jit(solution)/shard_map/all_to_all | solution.py:149
  68.9 1.3 %choose.1 = bf16[64,8,128]{2,1,0:T(8,128)(2,1)} custom-call(s32[192]{0:T(256)S(1)} %pad_add_fusion.parent.tables, bf16[64,8,128]{2,1,0:T(8,128)(2,1)S(1)} %all-to-all-done.pieces_ref), custom_call_target="tpu_custom_call" | custom-call | tf_op jit(solution)/shard_map/choose/pallas_call | solution.py:179
  70.2 5.8 %all-to-all-start.1 = ((bf16[64,8,128]{2,1,0:T(8,128)(2,1)}), bf16[64,8,128]{2,1,0:T(8,128)(2,1)S(1)}, u32[]{:S(2)}, u32[]{:S(2)}) async-start(bf16[64,8,128]{2,1,0:T(8,128)(2,1)} %choose.1), calls=%async_computation.1 | async-start | bytes 262144 | tf_op jit(solution)/shard_map/all_to_all | solution.py:149
  76.1 0.0 collective-permute-done.1.refs_1_
  76.1 0.0 collective-permute-done.2.refs_2_
  76.1 0.0 collective-permute-done.3.refs_3_
  76.1 0.0 copy-done
  76.1 8.7 %shard_map.82 = (f32[256,1024]{1,0:T(8,128)S(1)}, f32[256,128]{1,0:T(8,128)S(1)}) custom-call(bf16[256,1024]{1,0:T(8,128)(2,1)S(1)} %copy-done, bf16[2,768,128]{2,1,0:T(8,128)(2,1)S(1)} %pad_maximum_fusion.refs_0_, bf16[2,768,128]{2,1,0:T(8,128)(2,1)S(1)} %collective-permute-done.1.refs_1_, bf16[2,768,128]{2,1,0:T(8,128)(2,1)S(1)} %collective-permute-done.2.refs_2_, ...), custom_call_target="tpu_custom_call" | custom-call | flops 3489660928 | bytes 2752512 | tf_op jit(solution)/shard_map/pallas_call | solution.py:124
  84.8 1.6 %all-to-all-done.1 = bf16[64,8,128]{2,1,0:T(8,128)(2,1)S(1)} async-done(((bf16[64,8,128]{2,1,0:T(8,128)(2,1)}), bf16[64,8,128]{2,1,0:T(8,128)(2,1)S(1)}, u32[]{:S(2)}, u32[]{:S(2)}) %all-to-all-start.1) | async-done | bytes 131104 | tf_op jit(solution)/shard_map/all_to_all | solution.py:149
  86.5 3.1 %shard_map.83 = bf16[256,1024]{1,0:T(8,128)(2,1)} custom-call(s32[1]{0:T(128)} %bitcast.me, s32[192]{0:T(256)S(1)} %pad_add_fusion.parent.tables, bf16[256,1024]{1,0:T(8,128)(2,1)S(1)} %copy-done, bf16[512,128]{1,0:T(8,128)(2,1)S(1)} %bitcast.17, f32[256,1024]{1,0:T(8,128)S(1)} %get-tuple-element.7.acc_in, f32[256,128]{1,0:T(8,128)S(1)} %get-tuple-element.8.stat_in), custom_call_target="tpu_custom_call" | custom-call | flops 268435456 | bytes 1179648 | tf_op jit(solution)/shard_map/pallas_call | solution.py:124
  (8 shorter events, 0.2 us)
Async XLA Ops:
  32.0 9.2 %collective-permute-start = (bf16[768,128]{1,0:T(8,128)(2,1)S(1)}, bf16[768,128]{1,0:T(8,128)(2,1)S(1)}, u32[]{:S(2)}, u32[]{:S(2)}) collective-permute-start(bf16[768,128]{1,0:T(8,128)(2,1)S(1)} %constant_dynamic-update-slice_fusion), channel_id=1, source_target_pairs={{0,64},{64,0},{1,65},{65,1},{2,66},{66,2},{3,67},{67,3},{4,68},{68... | collective-permute-start | bytes 589832 | tf_op jit(solution)/shard_map/ppermute | solution.py:154
  41.2 11.6 %copy-start.1 = (bf16[256,128]{1,0:T(8,128)(2,1)S(1)}, bf16[256,128]{1,0:T(8,128)(2,1)}, u32[]{:S(2)}) copy-start(bf16[256,128]{1,0:T(8,128)(2,1)} %refs_5_.1) | copy-start | bytes 196612
  41.2 11.6 %copy-start.2 = (bf16[256,128]{1,0:T(8,128)(2,1)S(1)}, bf16[256,128]{1,0:T(8,128)(2,1)}, u32[]{:S(2)}) copy-start(bf16[256,128]{1,0:T(8,128)(2,1)} %refs_4_.1) | copy-start | bytes 196612
  41.3 34.8 %copy-start = (bf16[256,1024]{1,0:T(8,128)(2,1)S(1)}, bf16[256,1024]{1,0:T(8,128)(2,1)}, u32[]{:S(2)}) copy-start(bf16[256,1024]{1,0:T(8,128)(2,1)} %q_ref.3) | copy-start | bytes 1572868
  41.3 34.8 %collective-permute-start.1 = (bf16[2,768,128]{2,1,0:T(8,128)(2,1)S(1)}, bf16[2,768,128]{2,1,0:T(8,128)(2,1)S(1)}, u32[]{:S(2)}, u32[]{:S(2)}) collective-permute-start(bf16[2,768,128]{2,1,0:T(8,128)(2,1)S(1)} %pad_maximum_fusion.refs_0_), channel_id=1, source_target_pairs={{0,128},{128,256},{256,384},{384,0},{1,129},{129,257},{257,385},{3... | collective-permute-start | bytes 1179656 | tf_op jit(solution)/shard_map/ppermute | solution.py:154
  44.8 31.3 %collective-permute-start.2 = (bf16[2,768,128]{2,1,0:T(8,128)(2,1)S(1)}, bf16[2,768,128]{2,1,0:T(8,128)(2,1)S(1)}, u32[]{:S(2)}, u32[]{:S(2)}) collective-permute-start(bf16[2,768,128]{2,1,0:T(8,128)(2,1)S(1)} %pad_maximum_fusion.refs_0_), channel_id=1, source_target_pairs={{0,256},{128,384},{256,0},{384,128},{1,257},{129,385},{257,1},{385... | collective-permute-start | bytes 1179656 | tf_op jit(solution)/shard_map/ppermute | solution.py:154
  49.5 26.6 %collective-permute-start.3 = (bf16[2,768,128]{2,1,0:T(8,128)(2,1)S(1)}, bf16[2,768,128]{2,1,0:T(8,128)(2,1)S(1)}, u32[]{:S(2)}, u32[]{:S(2)}) collective-permute-start(bf16[2,768,128]{2,1,0:T(8,128)(2,1)S(1)} %pad_maximum_fusion.refs_0_), channel_id=1, source_target_pairs={{0,384},{128,0},{256,128},{384,256},{1,385},{129,1},{257,129},{385... | collective-permute-start | bytes 1179656 | tf_op jit(solution)/shard_map/ppermute | solution.py:154
  53.5 15.4 %all-to-all-start = ((bf16[64,8,128]{2,1,0:T(8,128)(2,1)}), bf16[64,8,128]{2,1,0:T(8,128)(2,1)S(1)}, u32[]{:S(2)}, u32[]{:S(2)}) async-start(bf16[64,8,128]{2,1,0:T(8,128)(2,1)} %maximum_bitcast_fusion), calls=%async_computation | async-start | bytes 262144 | tf_op jit(solution)/shard_map/all_to_all | solution.py:149
  58.6 0.7 copy-start.3
  58.6 0.7 copy-start.4
  58.6 0.7 copy-start.5
  70.2 16.3 %all-to-all-start.1 = ((bf16[64,8,128]{2,1,0:T(8,128)(2,1)}), bf16[64,8,128]{2,1,0:T(8,128)(2,1)S(1)}, u32[]{:S(2)}, u32[]{:S(2)}) async-start(bf16[64,8,128]{2,1,0:T(8,128)(2,1)} %choose.1), calls=%async_computation.1 | async-start | bytes 262144 | tf_op jit(solution)/shard_map/all_to_all | solution.py:149

commit v6 on v4

--- a/solution.py
+++ b/solution.py
@@ -44,7 +44,7 @@
 
 
 def lanes(first, count):
-    return pl.ds(pl.multiple_of(first * HEAD_DIM, HEAD_DIM), count * HEAD_DIM)
+    return slice(first * HEAD_DIM, (first + count) * HEAD_DIM)
 
 
 def stacked(ref, step):
@@ -56,27 +56,15 @@
     return [a[i * tok : (i + 1) * tok] for i in range(GROUP)]
 
 
-def store_state(state, acc_ref, stat_ref, step):
-    top, total, acc = (split_rows(a) for a in state)
-    heads = acc_ref.shape[1] // HEAD_DIM
-    stat = stat_ref[...]
-    lane = lax.broadcasted_iota(jnp.int32, stat.shape, 1)
+def store_state(state, out_ref, level_ref, step):
+    top, total, acc = state
+    levels = level_ref[...]
+    lane = lax.broadcasted_iota(jnp.int32, levels.shape, 1)
+    outs, own = split_rows(acc / total), split_rows(top * SCALE2 + jnp.log2(total))
     for i in range(GROUP):
-        head = step * GROUP + i
-        acc_ref[:, lanes(head, 1)] = acc[i]
-        stat = jnp.where(lane == head, top[i], stat)
-        stat = jnp.where(lane == heads + head, total[i], stat)
-    stat_ref[...] = stat
-
-
-def load_state(acc_ref, stat_ref, step):
-    heads = acc_ref.shape[1] // HEAD_DIM
-    stat = stat_ref[...]
-    lane = lax.broadcasted_iota(jnp.int32, stat.shape, 1)
-    pick = lambda j: jnp.sum(jnp.where(lane == j, stat, 0.0), axis=1, keepdims=True)
-    top = jnp.concatenate([pick(step * GROUP + i) for i in range(GROUP)], 0)
-    total = jnp.concatenate([pick(heads + step * GROUP + i) for i in range(GROUP)], 0)
-    return top, total, stacked(acc_ref, step)
+        out_ref[:, lanes(step * GROUP + i, 1)] = outs[i]
+        levels = jnp.where(lane == step * GROUP + i, own[i], levels)
+    level_ref[...] = levels
 
 
 def gather_rows(blocks, keys, values):
@@ -95,37 +83,44 @@
 
 
 def most_kernel(q_ref, *refs):
-    blocks, (own_k, own_v, acc_ref, stat_ref, keys, values) = refs[:-6], refs[-6:]
+    blocks, (own_k, own_v, out_ref, level_ref, keys, values) = refs[:-6], refs[-6:]
     tok, width = q_ref.shape
     gather_rows(blocks, keys, values)
-    stat_ref[...] = jnp.zeros_like(stat_ref)
-
-    @pl.loop(0, width // HEAD_DIM // GROUP)
-    def _(step):
+    level_ref[...] = jnp.zeros_like(level_ref)
+
+    for step in range(width // HEAD_DIM // GROUP):
         q = stacked(q_ref, step)
         shape = (q.shape[0], tok)
         row = lax.rem(lax.broadcasted_iota(jnp.int32, shape, 0), tok)
         causal = lax.broadcasted_iota(jnp.int32, shape, 1) <= row
         parts = chunks(keys, values) + [(own_k[...], own_v[...], causal)]
-        store_state(absorb(q, parts, None), acc_ref, stat_ref, step)
-
-
-def last_kernel(me, tables, q_ref, far_ref, above_ref, acc_in, stat_in, o_ref, keys, values):
+        store_state(absorb(q, parts, None), out_ref, level_ref, step)
+
+
+def last_kernel(me, tables, q_ref, above_ref, *refs):
+    far, (out_in, level_in, o_ref, keys, values) = refs[:-5], refs[-5:]
     tok, width = q_ref.shape
     count = tables.shape[0] // 3
     fork, live = tables[count + me[0]], tables[2 * count + me[0]]
-    gather_rows([far_ref], keys, values)
-
-    @pl.loop(0, width // HEAD_DIM // GROUP)
-    def _(step):
+    gather_rows(far, keys, values)
+    kept = lax.broadcasted_iota(jnp.int32, (tok, HEAD_DIM), 0) < live
+
+    for step in range(width // HEAD_DIM // GROUP):
         q = stacked(q_ref, step)
         seen = lax.broadcasted_iota(jnp.int32, (q.shape[0], tok), 1) < fork
-        parts = chunks(keys, values) + [(above_ref[:tok], above_ref[tok:], seen)]
-        _, total, acc = absorb(q, parts, load_state(acc_in, stat_in, step))
-        kept = lax.broadcasted_iota(jnp.int32, (tok, HEAD_DIM), 0) < live
-        for i, out in enumerate(split_rows(acc / total)):
+        parts = chunks(keys, values) if far else []
+        parts.append((above_ref[:tok], above_ref[tok:], seen))
+        peak, extra, more = absorb(q, parts, None)
+        peak = jnp.broadcast_to(peak * SCALE2, more.shape)
+        levels = level_in[...]
+        pick = lambda j: jnp.broadcast_to(levels[:, j : j + 1], (tok, HEAD_DIM))
+        level = jnp.concatenate([pick(step * GROUP + i) for i in range(GROUP)], 0)
+        top = jnp.maximum(level, peak)
+        old, new = jnp.exp2(level - top), jnp.exp2(peak - top)
+        out = (stacked(out_in, step) * old + more * new) / (old + extra * new)
+        for i, part in enumerate(split_rows(out)):
             at = lanes(step * GROUP + i, 1)
-            o_ref[:, at] = jnp.where(kept, out, 0.0).astype(o_ref.dtype)
+            o_ref[:, at] = jnp.where(kept, part, 0.0).astype(o_ref.dtype)
 
 
 def attention(kernel, tables, arrays, outs, keys, scratch_rows):
@@ -164,23 +159,18 @@
 def body(queries, branch_keys, branch_values, prompt_keys, prompt_values, parent, fork, lengths):
     tok, width = queries.shape
     rows = prompt_keys.shape[0]
-    ny, nz, nc, nb = (lax.axis_size(a) for a in ("y", "zh", "c", BRANCH))
+    ny, nh, nb = lax.axis_size("y"), lax.axis_size(HEAD), lax.axis_size(BRANCH)
     unit = 2 * tok // nb
     me = lax.axis_index(BRANCH).reshape(1)
-    first_core = lax.axis_index("c") == 0
     tables = jnp.concatenate([parent, fork, lengths])
 
-    both = jnp.stack([prompt_keys, prompt_values]).reshape(2, rows, nz, nc, HEAD_DIM)
-    kept = jnp.where(first_core, both[:, :, :, 0], both[:, :, :, 1])
-    given = jnp.where(first_core, both[:, :, :, 1], both[:, :, :, 0])
-    taken = shifted(given, "c", 1)
-    mine = jnp.concatenate([kept, taken], 1).transpose(2, 0, 1, 3)
-    mine = mine.reshape(nz, 2 * nc * rows, HEAD_DIM)
+    split = lambda a: a.reshape(rows, nh, HEAD_DIM).transpose(1, 0, 2)
+    mine = jnp.concatenate([split(prompt_keys), split(prompt_values)], 1)
     spread = jnp.broadcast_to(mine[None], (ny,) + mine.shape)
-    line = exchange(spread.reshape(ny * nz, 2 * nc * rows, HEAD_DIM), ("y", "zh"))
-    half = ny * nz * nc * rows
+    line = exchange(spread.reshape(ny * nh, 2 * rows, HEAD_DIM), ("y",) + HEAD)
+    half = ny * nh * rows
     part = lambda a: a.reshape(half, HEAD_DIM)
-    line = jnp.concatenate([part(line[:, : nc * rows]), part(line[:, nc * rows :])], 0)
+    line = jnp.concatenate([part(line[:, :rows]), part(line[:, rows:])], 0)
     other = shifted(line, "zl", 1)
     block = jnp.stack([line, other])
     near = [block, shifted(block, "x", 1), shifted(block, "x", -1)]
@@ -201,16 +191,19 @@
     )(tables, pieces)
     above = exchange(chosen, BRANCH).reshape(2 * tok, HEAD_DIM)
 
-    state = (
-        jax.ShapeDtypeStruct((tok, width), jnp.float32),
-        jax.ShapeDtypeStruct((tok, HEAD_DIM), jnp.float32),
-    )
+    wide = jax.ShapeDtypeStruct((tok, width), jnp.float32)
+    level = jax.ShapeDtypeStruct((tok, HEAD_DIM), jnp.float32)
     keys = len(near) * 2 * half
-    carried = attention(
-        most_kernel, (), (queries, *near, branch_keys, branch_values), state, keys + tok, keys
+    state = attention(
+        most_kernel,
+        (),
+        (queries, *near, branch_keys, branch_values),
+        (wide, level),
+        keys + tok,
+        keys,
     )
     out = jax.ShapeDtypeStruct((tok, width), jnp.bfloat16)
-    arrays = (queries, far, above, *carried)
+    arrays = (queries, above, far, *state)
     return attention(last_kernel, (me, tables), arrays, out, 2 * half + tok, 2 * half)
 
 

time: 90.9 us -> 88.3 us (0.971)
  starting transfers between devices: 29.1 us -> 27.1 us
  Pallas kernels: 14.6 us -> 12.9 us
  blocking collectives: 29.6 us -> 31 us
    ppermute x5 -> x4, starting transfers between devices: 17.4 us -> 15.5 us  [shifted(): return lax.ppermute(a, axis, [(i, (i + step) % n) for i in range(n)])]
    pallas_call x2, Pallas kernels: 13.3 us -> 11.6 us  [attention(): pl.pallas_call(kernel, out_shape=outs, in_specs=[smem] * len(tables) + [v...]
    all_to_all x1, blocking collectives: 29.6 us -> 31 us  [exchange(): return lax.all_to_all(a, axes, split_axis=0, concat_axis=0, tiled=True)]
    ppermute x5 -> x4, waiting for transfers between devices: 5.35 us -> 5.86 us  [shifted(): return lax.ppermute(a, axis, [(i, (i + step) % n) for i in range(n)])]
  transfers between devices with their start and end apart: 7 -> 6, of which waited for: 4 -> 3; matrix products, arithmetic and copies ran while one was open for 1% -> 1% of each run, Pallas kernels for 9% -> 9%
where the time goes in v6:
time: 88.3 us; the launch traced here: 87.8 us
  blocking collectives  31 us (35%)
  starting transfers between devices  27.1 us (31%)
  waiting for transfers between devices  14.8 us (17%)
  Pallas kernels  12.9 us (15%)
  local copies, waits for them, and re-layouts  0.97 us (1%)
    all_to_all x1, blocking collectives, exchange(): return lax.all_to_all(a, axes, split_axis=0, concat_axis=0, tiled=True)  31 us
    ppermute x4, starting transfers between devices, shifted(): return lax.ppermute(a, axis, [(i, (i + step) % n) for i in range(n)])  15.5 us
    pallas_call x2, Pallas kernels, attention(): pl.pallas_call(kernel, out_shape=outs, in_specs=[smem] * len(tables) + [v...  11.6 us
    all_to_all x2, starting transfers between devices, exchange(): return lax.all_to_all(a, axes, split_axis=0, concat_axis=0, tiled=True)  11.6 us
    all_to_all x2, waiting for transfers between devices, exchange(): return lax.all_to_all(a, axes, split_axis=0, concat_axis=0, tiled=True)  8.95 us
    ppermute x4, waiting for transfers between devices, shifted(): return lax.ppermute(a, axis, [(i, (i + step) % n) for i in range(n)])  5.86 us
  transfers between devices with their start and end apart: 6, of which 3 were waited for; matrix products, arithmetic and copies ran while one was open for 1% of the time, Pallas kernels for 9%

profile of v6, /device:TPU:8, one launch (start us, length us, event | category | flops | bytes accessed | tf_op | source)
XLA Modules:
  0.0 87.8 jit_solution(11648466486158079263)
XLA Ops:
  0.0 0.7 bitcast_bitcast_fusion
  0.8 31.0 %all_to_all.15 = bf16[64,12,128]{2,1,0:T(8,128)(2,1)S(1)} all-to-all(bf16[64,12,128]{2,1,0:T(8,128)(2,1)S(1)} %bitcast.18), channel_id=1, replica_groups=mesh['x'=4,'zl'=2,'y'=8,'zh'=4,'c'=2] {'y','zh','c'}, dimensions={0} | all-to-all | bytes 393216 | tf_op jit(solution)/shard_map/all_to_all | solution.py:151
  31.8 0.1 fusion
  32.0 3.4 %collective-permute-start = (bf16[768,128]{1,0:T(8,128)(2,1)S(1)}, bf16[768,128]{1,0:T(8,128)(2,1)S(1)}, u32[]{:S(2)}, u32[]{:S(2)}) collective-permute-start(bf16[768,128]{1,0:T(8,128)(2,1)S(1)} %constant_dynamic-update-slice_fusion), channel_id=1, source_target_pairs={{0,64},{64,0},{1,65},{65,1},{2,66},{66,2},{3,67},{67,3},{4,68},{68... | collective-permute-start | bytes 589832 | tf_op jit(solution)/shard_map/ppermute | solution.py:156
  35.4 5.9 %collective-permute-done = bf16[768,128]{1,0:T(8,128)(2,1)S(1)} collective-permute-done((bf16[768,128]{1,0:T(8,128)(2,1)S(1)}, bf16[768,128]{1,0:T(8,128)(2,1)S(1)}, u32[]{:S(2)}, u32[]{:S(2)}) %collective-permute-start) | collective-permute-done | bytes 196640 | tf_op jit(solution)/shard_map/ppermute | solution.py:156
  41.2 0.0 copy-start
  41.2 0.0 copy-start.1
  41.2 0.0 copy-start.3
  41.2 0.0 copy-start.4
  41.2 0.0 copy-start.5
  41.3 0.0 copy-start.2
  41.3 3.5 %collective-permute-start.2 = (bf16[2,768,128]{2,1,0:T(8,128)(2,1)S(1)}, bf16[2,768,128]{2,1,0:T(8,128)(2,1)S(1)}, u32[]{:S(2)}, u32[]{:S(2)}) collective-permute-start(bf16[2,768,128]{2,1,0:T(8,128)(2,1)S(1)} %pad_maximum_fusion.refs_0_), channel_id=1, source_target_pairs={{0,128},{128,256},{256,384},{384,0},{1,129},{129,257},{257,385},{3... | collective-permute-start | bytes 1179656 | tf_op jit(solution)/shard_map/ppermute | solution.py:156
  44.9 3.7 %collective-permute-start.3 = (bf16[2,768,128]{2,1,0:T(8,128)(2,1)S(1)}, bf16[2,768,128]{2,1,0:T(8,128)(2,1)S(1)}, u32[]{:S(2)}, u32[]{:S(2)}) collective-permute-start(bf16[2,768,128]{2,1,0:T(8,128)(2,1)S(1)} %pad_maximum_fusion.refs_0_), channel_id=1, source_target_pairs={{0,384},{128,0},{256,128},{384,256},{1,385},{129,1},{257,129},{385... | collective-permute-start | bytes 1179656 | tf_op jit(solution)/shard_map/ppermute | solution.py:156
  48.5 0.0 copy-done
  48.5 0.0 copy-done.1
  48.5 0.7 maximum_bitcast_fusion
  49.2 6.2 %all-to-all-start = ((bf16[64,8,128]{2,1,0:T(8,128)(2,1)}), bf16[64,8,128]{2,1,0:T(8,128)(2,1)S(1)}, u32[]{:S(2)}, u32[]{:S(2)}) async-start(bf16[64,8,128]{2,1,0:T(8,128)(2,1)} %maximum_bitcast_fusion), calls=%async_computation | async-start | bytes 262144 | tf_op jit(solution)/shard_map/all_to_all | solution.py:151
  55.5 5.0 %collective-permute-start.1 = (bf16[2,768,128]{2,1,0:T(8,128)(2,1)S(1)}, bf16[2,768,128]{2,1,0:T(8,128)(2,1)S(1)}, u32[]{:S(2)}, u32[]{:S(2)}) collective-permute-start(bf16[2,768,128]{2,1,0:T(8,128)(2,1)S(1)} %pad_maximum_fusion.refs_0_), channel_id=1, source_target_pairs={{0,256},{128,384},{256,0},{384,128},{1,257},{129,385},{257,1},{385... | collective-permute-start | bytes 1179656 | tf_op jit(solution)/shard_map/ppermute | solution.py:156
  60.4 0.0 copy-done.3
  60.5 0.0 copy-done.4
  60.5 0.0 copy-done.5
  60.5 0.1 pad_add_fusion.parent.tables
  60.6 5.4 %all-to-all-done.pieces_ref = bf16[64,8,128]{2,1,0:T(8,128)(2,1)S(1)} async-done(((bf16[64,8,128]{2,1,0:T(8,128)(2,1)}), bf16[64,8,128]{2,1,0:T(8,128)(2,1)S(1)}, u32[]{:S(2)}, u32[]{:S(2)}) %all-to-all-start) | async-done | bytes 131104 | tf_op jit(solution)/shard_map/all_to_all | solution.py:151
  65.9 1.3 %choose.1 = bf16[64,8,128]{2,1,0:T(8,128)(2,1)} custom-call(s32[192]{0:T(256)S(1)} %pad_add_fusion.parent.tables, bf16[64,8,128]{2,1,0:T(8,128)(2,1)S(1)} %all-to-all-done.pieces_ref), custom_call_target="tpu_custom_call" | custom-call | tf_op jit(solution)/shard_map/choose/pallas_call | solution.py:181
  67.2 5.3 %all-to-all-start.1 = ((bf16[64,8,128]{2,1,0:T(8,128)(2,1)}), bf16[64,8,128]{2,1,0:T(8,128)(2,1)S(1)}, u32[]{:S(2)}, u32[]{:S(2)}) async-start(bf16[64,8,128]{2,1,0:T(8,128)(2,1)} %choose.1), calls=%async_computation.1 | async-start | bytes 262144 | tf_op jit(solution)/shard_map/all_to_all | solution.py:151
  72.5 0.0 collective-permute-done.2.refs_1_
  72.5 0.0 collective-permute-done.3.refs_2_
  72.5 0.0 copy-done.2
  72.5 6.9 %shard_map.82 = (f32[256,1024]{1,0:T(8,128)S(1)}, f32[256,128]{1,0:T(8,128)S(1)}) custom-call(bf16[256,1024]{1,0:T(8,128)(2,1)S(1)} %copy-done.2, bf16[2,768,128]{2,1,0:T(8,128)(2,1)S(1)} %pad_maximum_fusion.refs_0_, bf16[2,768,128]{2,1,0:T(8,128)(2,1)S(1)} %collective-permute-done.2.refs_1_, bf16[2,768,128]{2,1,0:T(8,128)(2,1)S(1)} %collective-permute-done.3.refs_2_, ...), custom_call_target="tpu_custom_call" | custom-call | flops 2684354560 | bytes 2359296 | tf_op jit(solution)/shard_map/pallas_call | solution.py:130
  79.4 3.6 %all-to-all-done.1 = bf16[64,8,128]{2,1,0:T(8,128)(2,1)S(1)} async-done(((bf16[64,8,128]{2,1,0:T(8,128)(2,1)}), bf16[64,8,128]{2,1,0:T(8,128)(2,1)S(1)}, u32[]{:S(2)}, u32[]{:S(2)}) %all-to-all-start.1) | async-done | bytes 131104 | tf_op jit(solution)/shard_map/all_to_all | solution.py:151
  83.0 0.0 collective-permute-done.1.refs_0_
  83.0 4.8 %shard_map.83 = bf16[256,1024]{1,0:T(8,128)(2,1)} custom-call(s32[1]{0:T(128)} %bitcast.me, s32[192]{0:T(256)S(1)} %pad_add_fusion.parent.tables, bf16[256,1024]{1,0:T(8,128)(2,1)S(1)} %copy-done.2, bf16[512,128]{1,0:T(8,128)(2,1)S(1)} %bitcast.17, bf16[2,768,128]{2,1,0:T(8,128)(2,1)S(1)} %collective-permute-done.1.refs_0_, ...), custom_call_target="tpu_custom_call" | custom-call | flops 1073741824 | bytes 1572864 | tf_op jit(solution)/shard_map/pallas_call | solution.py:130
  (8 shorter events, 0.2 us)
Async XLA Ops:
  32.0 9.2 %collective-permute-start = (bf16[768,128]{1,0:T(8,128)(2,1)S(1)}, bf16[768,128]{1,0:T(8,128)(2,1)S(1)}, u32[]{:S(2)}, u32[]{:S(2)}) collective-permute-start(bf16[768,128]{1,0:T(8,128)(2,1)S(1)} %constant_dynamic-update-slice_fusion), channel_id=1, source_target_pairs={{0,64},{64,0},{1,65},{65,1},{2,66},{66,2},{3,67},{67,3},{4,68},{68... | collective-permute-start | bytes 589832 | tf_op jit(solution)/shard_map/ppermute | solution.py:156
  41.2 7.3 %copy-start = (bf16[256,128]{1,0:T(8,128)(2,1)S(1)}, bf16[256,128]{1,0:T(8,128)(2,1)}, u32[]{:S(2)}) copy-start(bf16[256,128]{1,0:T(8,128)(2,1)} %refs_4_.1) | copy-start | bytes 196612
  41.2 7.3 %copy-start.1 = (bf16[256,128]{1,0:T(8,128)(2,1)S(1)}, bf16[256,128]{1,0:T(8,128)(2,1)}, u32[]{:S(2)}) copy-start(bf16[256,128]{1,0:T(8,128)(2,1)} %refs_3_.1) | copy-start | bytes 196612
  41.2 19.2 %copy-start.3 = (s32[64]{0:T(128)S(1)}, s32[64]{0:T(128)}, u32[]{:S(2)}) copy-start(s32[64]{0:T(128)} %param.15) | copy-start | bytes 772
  41.2 19.2 %copy-start.4 = (s32[64]{0:T(128)S(1)}, s32[64]{0:T(128)}, u32[]{:S(2)}) copy-start(s32[64]{0:T(128)} %param.14) | copy-start | bytes 772
  41.2 19.2 %copy-start.5 = (s32[64]{0:T(128)S(1)}, s32[64]{0:T(128)}, u32[]{:S(2)}) copy-start(s32[64]{0:T(128)} %param.13) | copy-start | bytes 772
  41.3 31.2 %copy-start.2 = (bf16[256,1024]{1,0:T(8,128)(2,1)S(1)}, bf16[256,1024]{1,0:T(8,128)(2,1)}, u32[]{:S(2)}) copy-start(bf16[256,1024]{1,0:T(8,128)(2,1)} %q_ref.3) | copy-start | bytes 1572868
  41.3 31.2 %collective-permute-start.2 = (bf16[2,768,128]{2,1,0:T(8,128)(2,1)S(1)}, bf16[2,768,128]{2,1,0:T(8,128)(2,1)S(1)}, u32[]{:S(2)}, u32[]{:S(2)}) collective-permute-start(bf16[2,768,128]{2,1,0:T(8,128)(2,1)S(1)} %pad_maximum_fusion.refs_0_), channel_id=1, source_target_pairs={{0,128},{128,256},{256,384},{384,0},{1,129},{129,257},{257,385},{3... | collective-permute-start | bytes 1179656 | tf_op jit(solution)/shard_map/ppermute | solution.py:156
  44.9 27.7 %collective-permute-start.3 = (bf16[2,768,128]{2,1,0:T(8,128)(2,1)S(1)}, bf16[2,768,128]{2,1,0:T(8,128)(2,1)S(1)}, u32[]{:S(2)}, u32[]{:S(2)}) collective-permute-start(bf16[2,768,128]{2,1,0:T(8,128)(2,1)S(1)} %pad_maximum_fusion.refs_0_), channel_id=1, source_target_pairs={{0,384},{128,0},{256,128},{384,256},{1,385},{129,1},{257,129},{385... | collective-permute-start | bytes 1179656 | tf_op jit(solution)/shard_map/ppermute | solution.py:156
  49.2 16.7 %all-to-all-start = ((bf16[64,8,128]{2,1,0:T(8,128)(2,1)}), bf16[64,8,128]{2,1,0:T(8,128)(2,1)S(1)}, u32[]{:S(2)}, u32[]{:S(2)}) async-start(bf16[64,8,128]{2,1,0:T(8,128)(2,1)} %maximum_bitcast_fusion), calls=%async_computation | async-start | bytes 262144 | tf_op jit(solution)/shard_map/all_to_all | solution.py:151
  55.5 27.6 %collective-permute-start.1 = (bf16[2,768,128]{2,1,0:T(8,128)(2,1)S(1)}, bf16[2,768,128]{2,1,0:T(8,128)(2,1)S(1)}, u32[]{:S(2)}, u32[]{:S(2)}) collective-permute-start(bf16[2,768,128]{2,1,0:T(8,128)(2,1)S(1)} %pad_maximum_fusion.refs_0_), channel_id=1, source_target_pairs={{0,256},{128,384},{256,0},{384,128},{1,257},{129,385},{257,1},{385... | collective-permute-start | bytes 1179656 | tf_op jit(solution)/shard_map/ppermute | solution.py:156
  67.2 15.8 %all-to-all-start.1 = ((bf16[64,8,128]{2,1,0:T(8,128)(2,1)}), bf16[64,8,128]{2,1,0:T(8,128)(2,1)S(1)}, u32[]{:S(2)}, u32[]{:S(2)}) async-start(bf16[64,8,128]{2,1,0:T(8,128)(2,1)} %choose.1), calls=%async_computation.1 | async-start | bytes 262144 | tf_op jit(solution)/shard_map/all_to_all | solution.py:151

commit v7 on v6

--- a/solution.py
+++ b/solution.py
@@ -56,13 +56,27 @@
     return [a[i * tok : (i + 1) * tok] for i in range(GROUP)]
 
 
-def store_state(state, out_ref, level_ref, step):
-    top, total, acc = state
+def merged(state, mean_in, level_in, step):
+    peak, extra, more = state
+    peak = jnp.broadcast_to(peak * SCALE2, more.shape)
+    if mean_in is None:
+        return more / extra, peak + jnp.log2(extra)
+    tok = level_in.shape[0]
+    levels = level_in[...]
+    pick = lambda j: jnp.broadcast_to(levels[:, j : j + 1], (tok, HEAD_DIM))
+    level = jnp.concatenate([pick(step * GROUP + i) for i in range(GROUP)], 0)
+    top = jnp.maximum(level, peak)
+    old, new = jnp.exp2(level - top), jnp.exp2(peak - top)
+    total = old + extra * new
+    return (stacked(mean_in, step) * old + more * new) / total, top + jnp.log2(total)
+
+
+def store_state(mean, level, mean_ref, level_ref, step):
     levels = level_ref[...]
     lane = lax.broadcasted_iota(jnp.int32, levels.shape, 1)
-    outs, own = split_rows(acc / total), split_rows(top * SCALE2 + jnp.log2(total))
+    means, own = split_rows(mean), split_rows(level)
     for i in range(GROUP):
-        out_ref[:, lanes(step * GROUP + i, 1)] = outs[i]
+        mean_ref[:, lanes(step * GROUP + i, 1)] = means[i].astype(mean_ref.dtype)
         levels = jnp.where(lane == step * GROUP + i, own[i], levels)
     level_ref[...] = levels
 
@@ -82,42 +96,41 @@
     return [(keys[i : i + CHUNK], values[i : i + CHUNK], None) for i in ends]
 
 
-def most_kernel(q_ref, *refs):
-    blocks, (own_k, own_v, out_ref, level_ref, keys, values) = refs[:-6], refs[-6:]
+def own_kernel(q_ref, block, own_k, own_v, mean_ref, level_ref, keys, values):
     tok, width = q_ref.shape
-    gather_rows(blocks, keys, values)
+    gather_rows([block], keys, values)
     level_ref[...] = jnp.zeros_like(level_ref)
-
     for step in range(width // HEAD_DIM // GROUP):
         q = stacked(q_ref, step)
         shape = (q.shape[0], tok)
         row = lax.rem(lax.broadcasted_iota(jnp.int32, shape, 0), tok)
         causal = lax.broadcasted_iota(jnp.int32, shape, 1) <= row
         parts = chunks(keys, values) + [(own_k[...], own_v[...], causal)]
-        store_state(absorb(q, parts, None), out_ref, level_ref, step)
-
-
-def last_kernel(me, tables, q_ref, above_ref, *refs):
-    far, (out_in, level_in, o_ref, keys, values) = refs[:-5], refs[-5:]
+        mean, level = merged(absorb(q, parts, None), None, None, step)
+        store_state(mean, level, mean_ref, level_ref, step)
+
+
+def most_kernel(q_ref, left, right, mean_in, level_in, mean_ref, level_ref, keys, values):
+    _, width = q_ref.shape
+    gather_rows([left, right], keys, values)
+    level_ref[...] = jnp.zeros_like(level_ref)
+    for step in range(width // HEAD_DIM // GROUP):
+        state = absorb(stacked(q_ref, step), chunks(keys, values), None)
+        mean, level = merged(state, mean_in, level_in, step)
+        store_state(mean, level, mean_ref, level_ref, step)
+
+
+def last_kernel(me, tables, q_ref, above_ref, far, mean_in, level_in, o_ref, keys, values):
     tok, width = q_ref.shape
     count = tables.shape[0] // 3
     fork, live = tables[count + me[0]], tables[2 * count + me[0]]
-    gather_rows(far, keys, values)
+    gather_rows([far], keys, values)
     kept = lax.broadcasted_iota(jnp.int32, (tok, HEAD_DIM), 0) < live
-
     for step in range(width // HEAD_DIM // GROUP):
         q = stacked(q_ref, step)
         seen = lax.broadcasted_iota(jnp.int32, (q.shape[0], tok), 1) < fork
-        parts = chunks(keys, values) if far else []
-        parts.append((above_ref[:tok], above_ref[tok:], seen))
-        peak, extra, more = absorb(q, parts, None)
-        peak = jnp.broadcast_to(peak * SCALE2, more.shape)
-        levels = level_in[...]
-        pick = lambda j: jnp.broadcast_to(levels[:, j : j + 1], (tok, HEAD_DIM))
-        level = jnp.concatenate([pick(step * GROUP + i) for i in range(GROUP)], 0)
-        top = jnp.maximum(level, peak)
-        old, new = jnp.exp2(level - top), jnp.exp2(peak - top)
-        out = (stacked(out_in, step) * old + more * new) / (old + extra * new)
+        parts = chunks(keys, values) + [(above_ref[:tok], above_ref[tok:], seen)]
+        out, _ = merged(absorb(q, parts, None), mean_in, level_in, step)
         for i, part in enumerate(split_rows(out)):
             at = lanes(step * GROUP + i, 1)
             o_ref[:, at] = jnp.where(kept, part, 0.0).astype(o_ref.dtype)
@@ -173,7 +186,7 @@
     line = jnp.concatenate([part(line[:, :rows]), part(line[:, rows:])], 0)
     other = shifted(line, "zl", 1)
     block = jnp.stack([line, other])
-    near = [block, shifted(block, "x", 1), shifted(block, "x", -1)]
+    near = [shifted(block, "x", 1), shifted(block, "x", -1)]
     far = shifted(block, "x", 2)
 
     own = jnp.concatenate([branch_keys, branch_values], 0).reshape(nb, unit, HEAD_DIM)
@@ -193,18 +206,15 @@
 
     wide = jax.ShapeDtypeStruct((tok, width), jnp.float32)
     level = jax.ShapeDtypeStruct((tok, HEAD_DIM), jnp.float32)
-    keys = len(near) * 2 * half
-    state = attention(
-        most_kernel,
-        (),
-        (queries, *near, branch_keys, branch_values),
-        (wide, level),
-        keys + tok,
-        keys,
-    )
+    narrow = jax.ShapeDtypeStruct((tok, width), jnp.bfloat16)
+    keys = 2 * half
+    arrays = (queries, block, branch_keys, branch_values)
+    state = attention(own_kernel, (), arrays, (narrow, level), keys + tok, keys)
+    arrays = (queries, *near, *state)
+    state = attention(most_kernel, (), arrays, (wide, level), 2 * keys, 2 * keys)
     out = jax.ShapeDtypeStruct((tok, width), jnp.bfloat16)
     arrays = (queries, above, far, *state)
-    return attention(last_kernel, (me, tables), arrays, out, 2 * half + tok, 2 * half)
+    return attention(last_kernel, (me, tables), arrays, out, keys + tok, keys)
 
 
 def solution(mesh):

time: 88.3 us -> 88.3 us (level)
  Pallas kernels: 12.9 us -> 13.8 us
  waiting for transfers between devices: 14.8 us -> 13.9 us
    all_to_all x2, waiting for transfers between devices: 8.95 us -> 8.04 us  [exchange(): return lax.all_to_all(a, axes, split_axis=0, concat_axis=0, tiled=True)]
    pallas_call x2 -> x3, Pallas kernels: 11.6 us -> 12.5 us  [attention(): pl.pallas_call(kernel, out_shape=outs, in_specs=[smem] * len(tables) + [v...]
  transfers between devices with their start and end apart: 6 -> 6, of which waited for: 3 -> 3; matrix products, arithmetic and copies ran while one was open for 1% -> 1% of each run, Pallas kernels for 9% -> 10%
where the time goes in v7:
time: 88.3 us; the launch traced here: 87.8 us
  blocking collectives  31 us (35%)
  starting transfers between devices  27.1 us (31%)
  waiting for transfers between devices  13.9 us (16%)
  Pallas kernels  13.8 us (16%)
  local copies, waits for them, and re-layouts  0.97 us (1%)
    all_to_all x1, blocking collectives, exchange(): return lax.all_to_all(a, axes, split_axis=0, concat_axis=0, tiled=True)  31 us
    ppermute x4, starting transfers between devices, shifted(): return lax.ppermute(a, axis, [(i, (i + step) % n) for i in range(n)])  15.5 us
    pallas_call x3, Pallas kernels, attention(): pl.pallas_call(kernel, out_shape=outs, in_specs=[smem] * len(tables) + [v...  12.5 us
    all_to_all x2, starting transfers between devices, exchange(): return lax.all_to_all(a, axes, split_axis=0, concat_axis=0, tiled=True)  11.6 us
    all_to_all x2, waiting for transfers between devices, exchange(): return lax.all_to_all(a, axes, split_axis=0, concat_axis=0, tiled=True)  8.04 us
    ppermute x4, waiting for transfers between devices, shifted(): return lax.ppermute(a, axis, [(i, (i + step) % n) for i in range(n)])  5.86 us
  transfers between devices with their start and end apart: 6, of which 3 were waited for; matrix products, arithmetic and copies ran while one was open for 1% of the time, Pallas kernels for 10%

profile of v7, /device:TPU:8, one launch (start us, length us, event | category | flops | bytes accessed | tf_op | source)
XLA Modules:
  0.0 87.8 jit_solution(17400605584479929258)
XLA Ops:
  0.0 0.7 bitcast_bitcast_fusion
  0.8 31.0 %all_to_all.15 = bf16[64,12,128]{2,1,0:T(8,128)(2,1)S(1)} all-to-all(bf16[64,12,128]{2,1,0:T(8,128)(2,1)S(1)} %bitcast.18), channel_id=1, replica_groups=mesh['x'=4,'zl'=2,'y'=8,'zh'=4,'c'=2] {'y','zh','c'}, dimensions={0} | all-to-all | bytes 393216 | tf_op jit(solution)/shard_map/all_to_all | solution.py:164
  31.8 0.1 fusion
  32.0 3.4 %collective-permute-start = (bf16[768,128]{1,0:T(8,128)(2,1)S(1)}, bf16[768,128]{1,0:T(8,128)(2,1)S(1)}, u32[]{:S(2)}, u32[]{:S(2)}) collective-permute-start(bf16[768,128]{1,0:T(8,128)(2,1)S(1)} %constant_dynamic-update-slice_fusion), channel_id=1, source_target_pairs={{0,64},{64,0},{1,65},{65,1},{2,66},{66,2},{3,67},{67,3},{4,68},{68... | collective-permute-start | bytes 589832 | tf_op jit(solution)/shard_map/ppermute | solution.py:169
  35.4 5.9 %collective-permute-done = bf16[768,128]{1,0:T(8,128)(2,1)S(1)} collective-permute-done((bf16[768,128]{1,0:T(8,128)(2,1)S(1)}, bf16[768,128]{1,0:T(8,128)(2,1)S(1)}, u32[]{:S(2)}, u32[]{:S(2)}) %collective-permute-start) | collective-permute-done | bytes 196640 | tf_op jit(solution)/shard_map/ppermute | solution.py:169
  41.2 0.0 copy-start
  41.2 0.0 copy-start.1
  41.2 0.0 copy-start.3
  41.2 0.0 copy-start.4
  41.2 0.0 copy-start.5
  41.3 0.0 copy-start.2
  41.3 3.5 %collective-permute-start.2 = (bf16[2,768,128]{2,1,0:T(8,128)(2,1)S(1)}, bf16[2,768,128]{2,1,0:T(8,128)(2,1)S(1)}, u32[]{:S(2)}, u32[]{:S(2)}) collective-permute-start(bf16[2,768,128]{2,1,0:T(8,128)(2,1)S(1)} %pad_maximum_fusion.block), channel_id=1, source_target_pairs={{0,128},{128,256},{256,384},{384,0},{1,129},{129,257},{257,385},{3... | collective-permute-start | bytes 1179656 | tf_op jit(solution)/shard_map/ppermute | solution.py:169
  44.9 3.7 %collective-permute-start.3 = (bf16[2,768,128]{2,1,0:T(8,128)(2,1)S(1)}, bf16[2,768,128]{2,1,0:T(8,128)(2,1)S(1)}, u32[]{:S(2)}, u32[]{:S(2)}) collective-permute-start(bf16[2,768,128]{2,1,0:T(8,128)(2,1)S(1)} %pad_maximum_fusion.block), channel_id=1, source_target_pairs={{0,384},{128,0},{256,128},{384,256},{1,385},{129,1},{257,129},{385... | collective-permute-start | bytes 1179656 | tf_op jit(solution)/shard_map/ppermute | solution.py:169
  48.5 0.0 copy-done
  48.5 0.0 copy-done.1
  48.5 0.7 maximum_bitcast_fusion
  49.2 6.2 %all-to-all-start = ((bf16[64,8,128]{2,1,0:T(8,128)(2,1)}), bf16[64,8,128]{2,1,0:T(8,128)(2,1)S(1)}, u32[]{:S(2)}, u32[]{:S(2)}) async-start(bf16[64,8,128]{2,1,0:T(8,128)(2,1)} %maximum_bitcast_fusion), calls=%async_computation | async-start | bytes 262144 | tf_op jit(solution)/shard_map/all_to_all | solution.py:164
  55.5 5.0 %collective-permute-start.1 = (bf16[2,768,128]{2,1,0:T(8,128)(2,1)S(1)}, bf16[2,768,128]{2,1,0:T(8,128)(2,1)S(1)}, u32[]{:S(2)}, u32[]{:S(2)}) collective-permute-start(bf16[2,768,128]{2,1,0:T(8,128)(2,1)S(1)} %pad_maximum_fusion.block), channel_id=1, source_target_pairs={{0,256},{128,384},{256,0},{384,128},{1,257},{129,385},{257,1},{385... | collective-permute-start | bytes 1179656 | tf_op jit(solution)/shard_map/ppermute | solution.py:169
  60.4 0.0 copy-done.3
  60.5 0.0 copy-done.4
  60.5 0.0 copy-done.5
  60.5 0.1 pad_add_fusion.parent.tables
  60.6 5.4 %all-to-all-done.pieces_ref = bf16[64,8,128]{2,1,0:T(8,128)(2,1)S(1)} async-done(((bf16[64,8,128]{2,1,0:T(8,128)(2,1)}), bf16[64,8,128]{2,1,0:T(8,128)(2,1)S(1)}, u32[]{:S(2)}, u32[]{:S(2)}) %all-to-all-start) | async-done | bytes 131104 | tf_op jit(solution)/shard_map/all_to_all | solution.py:164
  65.9 1.3 %choose.1 = bf16[64,8,128]{2,1,0:T(8,128)(2,1)} custom-call(s32[192]{0:T(256)S(1)} %pad_add_fusion.parent.tables, bf16[64,8,128]{2,1,0:T(8,128)(2,1)S(1)} %all-to-all-done.pieces_ref), custom_call_target="tpu_custom_call" | custom-call | tf_op jit(solution)/shard_map/choose/pallas_call | solution.py:194
  67.2 5.3 %all-to-all-start.1 = ((bf16[64,8,128]{2,1,0:T(8,128)(2,1)}), bf16[64,8,128]{2,1,0:T(8,128)(2,1)S(1)}, u32[]{:S(2)}, u32[]{:S(2)}) async-start(bf16[64,8,128]{2,1,0:T(8,128)(2,1)} %choose.1), calls=%async_computation.1 | async-start | bytes 262144 | tf_op jit(solution)/shard_map/all_to_all | solution.py:164
  72.5 0.0 copy-done.2
  72.5 3.0 %shard_map.82 = (bf16[256,1024]{1,0:T(8,128)(2,1)S(1)}, f32[256,128]{1,0:T(8,128)S(1)}) custom-call(bf16[256,1024]{1,0:T(8,128)(2,1)S(1)} %copy-done.2, bf16[2,768,128]{2,1,0:T(8,128)(2,1)S(1)} %pad_maximum_fusion.block, bf16[256,128]{1,0:T(8,128)(2,1)S(1)} %copy-done.1, bf16[256,128]{1,0:T(8,128)(2,1)S(1)} %copy-done), custom_call_target="tpu_custom_call" | custom-call | flops 1073741824 | bytes 1572864 | tf_op jit(solution)/shard_map/pallas_call | solution.py:143
  75.6 0.0 collective-permute-done.2.left
  75.6 0.0 collective-permute-done.3.right
  75.6 4.7 %shard_map.83 = (f32[256,1024]{1,0:T(8,128)S(1)}, f32[256,128]{1,0:T(8,128)S(1)}) custom-call(bf16[256,1024]{1,0:T(8,128)(2,1)S(1)} %copy-done.2, bf16[2,768,128]{2,1,0:T(8,128)(2,1)S(1)} %collective-permute-done.2.left, bf16[2,768,128]{2,1,0:T(8,128)(2,1)S(1)} %collective-permute-done.3.right, bf16[256,1024]{1,0:T(8,128)(2,1)S(1)} %get-tuple-element.9.mean_in, ...), custom_call_target="tpu_custom_call" | custom-call | flops 1610612736 | bytes 1835008 | tf_op jit(solution)/shard_map/pallas_call | solution.py:143
  80.3 2.7 %all-to-all-done.1 = bf16[64,8,128]{2,1,0:T(8,128)(2,1)S(1)} async-done(((bf16[64,8,128]{2,1,0:T(8,128)(2,1)}), bf16[64,8,128]{2,1,0:T(8,128)(2,1)S(1)}, u32[]{:S(2)}, u32[]{:S(2)}) %all-to-all-start.1) | async-done | bytes 131104 | tf_op jit(solution)/shard_map/all_to_all | solution.py:164
  83.0 0.0 collective-permute-done.1.far
  83.0 4.7 %shard_map.84 = bf16[256,1024]{1,0:T(8,128)(2,1)} custom-call(s32[1]{0:T(128)} %bitcast.me, s32[192]{0:T(256)S(1)} %pad_add_fusion.parent.tables, bf16[256,1024]{1,0:T(8,128)(2,1)S(1)} %copy-done.2, bf16[512,128]{1,0:T(8,128)(2,1)S(1)} %bitcast.17, bf16[2,768,128]{2,1,0:T(8,128)(2,1)S(1)} %collective-permute-done.1.far, ...), custom_call_target="tpu_custom_call" | custom-call | flops 1073741824 | bytes 1572864 | tf_op jit(solution)/shard_map/pallas_call | solution.py:143
  (8 shorter events, 0.2 us)
Async XLA Ops:
  32.0 9.2 %collective-permute-start = (bf16[768,128]{1,0:T(8,128)(2,1)S(1)}, bf16[768,128]{1,0:T(8,128)(2,1)S(1)}, u32[]{:S(2)}, u32[]{:S(2)}) collective-permute-start(bf16[768,128]{1,0:T(8,128)(2,1)S(1)} %constant_dynamic-update-slice_fusion), channel_id=1, source_target_pairs={{0,64},{64,0},{1,65},{65,1},{2,66},{66,2},{3,67},{67,3},{4,68},{68... | collective-permute-start | bytes 589832 | tf_op jit(solution)/shard_map/ppermute | solution.py:169
  41.2 7.3 %copy-start = (bf16[256,128]{1,0:T(8,128)(2,1)S(1)}, bf16[256,128]{1,0:T(8,128)(2,1)}, u32[]{:S(2)}) copy-start(bf16[256,128]{1,0:T(8,128)(2,1)} %own_v.1) | copy-start | bytes 196612
  41.2 7.3 %copy-start.1 = (bf16[256,128]{1,0:T(8,128)(2,1)S(1)}, bf16[256,128]{1,0:T(8,128)(2,1)}, u32[]{:S(2)}) copy-start(bf16[256,128]{1,0:T(8,128)(2,1)} %own_k.1) | copy-start | bytes 196612
  41.2 19.2 %copy-start.3 = (s32[64]{0:T(128)S(1)}, s32[64]{0:T(128)}, u32[]{:S(2)}) copy-start(s32[64]{0:T(128)} %param.15) | copy-start | bytes 772
  41.2 19.2 %copy-start.4 = (s32[64]{0:T(128)S(1)}, s32[64]{0:T(128)}, u32[]{:S(2)}) copy-start(s32[64]{0:T(128)} %param.14) | copy-start | bytes 772
  41.2 19.2 %copy-start.5 = (s32[64]{0:T(128)S(1)}, s32[64]{0:T(128)}, u32[]{:S(2)}) copy-start(s32[64]{0:T(128)} %param.13) | copy-start | bytes 772
  41.3 31.2 %copy-start.2 = (bf16[256,1024]{1,0:T(8,128)(2,1)S(1)}, bf16[256,1024]{1,0:T(8,128)(2,1)}, u32[]{:S(2)}) copy-start(bf16[256,1024]{1,0:T(8,128)(2,1)} %q_ref.5) | copy-start | bytes 1572868
  41.3 34.3 %collective-permute-start.2 = (bf16[2,768,128]{2,1,0:T(8,128)(2,1)S(1)}, bf16[2,768,128]{2,1,0:T(8,128)(2,1)S(1)}, u32[]{:S(2)}, u32[]{:S(2)}) collective-permute-start(bf16[2,768,128]{2,1,0:T(8,128)(2,1)S(1)} %pad_maximum_fusion.block), channel_id=1, source_target_pairs={{0,128},{128,256},{256,384},{384,0},{1,129},{129,257},{257,385},{3... | collective-permute-start | bytes 1179656 | tf_op jit(solution)/shard_map/ppermute | solution.py:169
  44.9 30.7 %collective-permute-start.3 = (bf16[2,768,128]{2,1,0:T(8,128)(2,1)S(1)}, bf16[2,768,128]{2,1,0:T(8,128)(2,1)S(1)}, u32[]{:S(2)}, u32[]{:S(2)}) collective-permute-start(bf16[2,768,128]{2,1,0:T(8,128)(2,1)S(1)} %pad_maximum_fusion.block), channel_id=1, source_target_pairs={{0,384},{128,0},{256,128},{384,256},{1,385},{129,1},{257,129},{385... | collective-permute-start | bytes 1179656 | tf_op jit(solution)/shard_map/ppermute | solution.py:169
  49.2 16.7 %all-to-all-start = ((bf16[64,8,128]{2,1,0:T(8,128)(2,1)}), bf16[64,8,128]{2,1,0:T(8,128)(2,1)S(1)}, u32[]{:S(2)}, u32[]{:S(2)}) async-start(bf16[64,8,128]{2,1,0:T(8,128)(2,1)} %maximum_bitcast_fusion), calls=%async_computation | async-start | bytes 262144 | tf_op jit(solution)/shard_map/all_to_all | solution.py:164
  55.5 27.6 %collective-permute-start.1 = (bf16[2,768,128]{2,1,0:T(8,128)(2,1)S(1)}, bf16[2,768,128]{2,1,0:T(8,128)(2,1)S(1)}, u32[]{:S(2)}, u32[]{:S(2)}) collective-permute-start(bf16[2,768,128]{2,1,0:T(8,128)(2,1)S(1)} %pad_maximum_fusion.block), channel_id=1, source_target_pairs={{0,256},{128,384},{256,0},{384,128},{1,257},{129,385},{257,1},{385... | collective-permute-start | bytes 1179656 | tf_op jit(solution)/shard_map/ppermute | solution.py:169
  67.2 15.8 %all-to-all-start.1 = ((bf16[64,8,128]{2,1,0:T(8,128)(2,1)}), bf16[64,8,128]{2,1,0:T(8,128)(2,1)S(1)}, u32[]{:S(2)}, u32[]{:S(2)}) async-start(bf16[64,8,128]{2,1,0:T(8,128)(2,1)} %choose.1), calls=%async_computation.1 | async-start | bytes 262144 | tf_op jit(solution)/shard_map/all_to_all | solution.py:164
